TPU v7x, 32 devices: a whole 2x2x4 slice. The times are simulated.
32 devices in a mesh: groups: 2 (over y), row: 4 (over z), col: 4 (over x, core).
Axes of the slice: x: 2, y: 2, z: 4, core: 2. Of those that a mesh axis runs over, the one named last changes fastest.
Arguments:
- raw_files: bfloat16 [128, 4, 8, 12000], P(('groups', 'row'), 'col'), parts along dimension 0
- file_channels: int32 [128, 4], P(('groups', 'row'), 'col'), parts along dimension 0, may hold values from 0 to 255, as said below
- reader_counts: int32 [8, 4], P(('groups', 'row'), 'col'), parts along dimension 0, may hold values from 0 to 16, as said below
- fir_taps: float32 [32], replicated, may hold values from -1 to 1
- band_bins: int32 [64], replicated, may hold values from 1 to 1499, as said below
Outputs:
- stack: bfloat16 [512, 4, 64, 128], P(('groups', 'row'), 'col'), parts along dimension 0
There are 2 independent parts, one for each index of `groups`. A program takes and returns all parts, laid end to end along the dimension named above; an argument that names none is the same for every part. Nothing has to cross between parts.
Inputs may be any that keep to these rules, and one draw needn't show every extreme that they name: `file_channels`: channel q belongs to owner row q // 64, column (q // 16) % 4. Every channel stands in exactly one live slot (slot below its reader's count), of a reader in its owner's column. Live slots of one reader name at most 4 channels of one owner; in every column some reader holds exactly 4 channels of every owner. Slots at or above the count hold arbitrary channel numbers. `reader_counts`: in every column some reader holds 16 live slots. `band_bins`: Distinct.
All inputs are finite; a program needn't handle non-finite values.
Results may differ from a plain program's by a relative error of at most 0.017.
Values may be sent and summed in bfloat16 or wider, within the bound.
No kernel may reach another device: no remote copies, remote signals or barrier semaphores. Data moves between devices by JAX's collectives and lax.ppermute only.
A program may use at most 64 MiB of HBM per device.

v0:
```python
import math

import jax
import jax.numpy as jnp
from jax import lax
from jax.sharding import PartitionSpec as P

CH_DEV = 16
DEC = 4


def decimate(signal, fir_taps):
    count, records, samples = signal.shape
    length = samples // DEC
    taps = fir_taps.shape[0]
    outputs = 128
    span = outputs * DEC
    blocks = (length + outputs - 1) // outputs
    total = (blocks + 1) * span
    padded = jnp.pad(signal, ((0, 0), (0, 0), (0, total - samples)))
    leading = padded[:, :, : blocks * span].reshape(count, records, blocks, span)
    following = padded[:, :, span:].reshape(count, records, blocks, span)[:, :, :, : taps - DEC]
    window = jnp.concatenate([leading, following], axis=3)
    positions = jnp.arange(span + taps - DEC, dtype=jnp.int32)[:, None]
    columns = jnp.arange(outputs, dtype=jnp.int32)[None, :]
    offset = positions - DEC * columns
    banded = jnp.zeros((span + taps - DEC, outputs), jnp.float32)
    for index in range(taps):
        banded = banded + jnp.where(offset == index, fir_taps[index], jnp.float32(0.0))
    upper = banded.astype(jnp.bfloat16)
    lower = (banded - upper.astype(jnp.float32)).astype(jnp.bfloat16)
    result = jnp.einsum("iqbw,wn->iqbn", window, upper, preferred_element_type=jnp.float32)
    result = result + jnp.einsum("iqbw,wn->iqbn", window, lower, preferred_element_type=jnp.float32)
    return result.reshape(count, records, blocks * outputs)[:, :, :length].astype(jnp.bfloat16)


def whiten(signal, fir_taps, band_bins):
    count, records, samples = signal.shape
    length = samples // DEC
    decimated = decimate(signal, fir_taps)
    steps = jnp.arange(length, dtype=jnp.int32)
    product = band_bins[None, :] * steps[:, None] % length
    angle = 2.0 * math.pi / length * product.astype(jnp.float32)
    table = jnp.concatenate([jnp.cos(angle), -jnp.sin(angle)], axis=1).astype(jnp.bfloat16)
    spectra = jnp.dot(
        decimated.reshape(count * records, length), table, preferred_element_type=jnp.float32
    )
    power = jnp.mean(spectra * spectra, axis=1, keepdims=True)
    white = spectra / jnp.sqrt(power + 1e-06)
    return white.reshape(count, records, table.shape[1]).astype(jnp.bfloat16)


def slot_plan(file_channels, reader_counts, nrows, ncols, capacity):
    channels = file_channels[:, 0]
    slots = channels.shape[0]
    order = jnp.arange(slots, dtype=jnp.int32)
    live = order < reader_counts[0, 0]
    owner = channels // (CH_DEV * ncols)
    place = channels % CH_DEV
    earlier = (owner[None, :] == owner[:, None]) & live[None, :] & (order[None, :] < order[:, None])
    rank = jnp.sum(earlier.astype(jnp.int32), axis=1)
    where_to = jnp.where(live, owner * capacity + rank, -1)
    target = jnp.arange(nrows * capacity, dtype=jnp.int32)
    match = (where_to[None, :] == target[:, None]).astype(jnp.int32)
    filled = jnp.sum(match, axis=1) > 0
    source = jnp.sum(match * order[None, :], axis=1)
    label = jnp.where(filled, jnp.sum(match * place[None, :], axis=1), -1)
    return (source, filled, label)


def pack(data, source, filled, nrows, capacity):
    chosen = jnp.where(filled[:, None, None], data[source], jnp.zeros((), data.dtype))
    return chosen.reshape((nrows, capacity) + data.shape[1:])


def settle(received, labels):
    flat = received.reshape((-1,) + received.shape[2:])
    marks = labels.reshape(-1).astype(jnp.int32)
    total = marks.shape[0]
    match = (marks[None, :] == jnp.arange(CH_DEV, dtype=jnp.int32)[:, None]).astype(jnp.int32)
    source = jnp.sum(match * jnp.arange(total, dtype=jnp.int32)[None, :], axis=1)
    return flat[source]


def on_device(raw_files, file_channels, reader_counts, fir_taps, band_bins):
    nrows = lax.axis_size("row")
    ncols = lax.axis_size("col")
    capacity = max(2, (CH_DEV + nrows - 1) // nrows)
    source, filled, label = slot_plan(file_channels, reader_counts, nrows, ncols, capacity)
    labels = label.reshape(nrows, capacity).astype(jnp.bfloat16)
    reader_white = whiten(raw_files[:, 0], fir_taps, band_bins)
    outgoing = pack(reader_white, source, filled, nrows, capacity)
    arrived, arrived_labels = (
        lax.all_to_all(outgoing, "row", split_axis=0, concat_axis=0, tiled=True),
        lax.all_to_all(labels, "row", split_axis=0, concat_axis=0, tiled=True),
    )
    white_own = settle(arrived, arrived_labels)
    records = white_own.shape[1]
    width = white_own.shape[2] // 2
    row_white = lax.all_gather(white_own, "col", axis=0, tiled=True)
    left_count = row_white.shape[0]
    left = (
        row_white.reshape(left_count, records, 2, width)
        .transpose(0, 2, 1, 3)
        .reshape(left_count, 2 * records, width)
    )
    piece = lax.all_gather(white_own, "row", axis=0, tiled=True)
    right_count = piece.shape[0]
    split_piece = piece.reshape(right_count, records, 2, width)
    piece_re = split_piece[:, :, 0, :]
    piece_im = split_piece[:, :, 1, :]
    right_real = jnp.concatenate([piece_re, piece_im], axis=1)
    right_imag = jnp.concatenate([-piece_im, piece_re], axis=1)
    real = jnp.einsum("ikb,jkb->ijb", left, right_real, preferred_element_type=jnp.float32)
    imag = jnp.einsum("ikb,jkb->ijb", left, right_imag, preferred_element_type=jnp.float32)
    stacked = (jnp.concatenate([real, imag], axis=2) / records).astype(jnp.bfloat16)
    return stacked[:, None, :, :]


def solution(mesh):
    return jax.shard_map(
        on_device,
        mesh=mesh,
        in_specs=(
            P(("groups", "row"), "col", None, None),
            P(("groups", "row"), "col"),
            P(("groups", "row"), "col"),
            P(),
            P(),
        ),
        out_specs=P(("groups", "row"), "col", None, None),
        check_vma=False,
    )
```

profile of v0, /device:TPU:0, one launch (start us, length us, event | category | flops | bytes accessed | tf_op | source)
XLA Modules:
  0.0 111.3 jit_solution(5888975628344206008)
XLA Ops:
  0.0 0.7 and_select_fusion.2
  0.7 0.7 fusion.64
  2.0 0.2 convert_reduce_fusion.1
  2.2 0.1 select_reduce_fusion.1
  2.3 0.7 convert_element_type.76
  3.0 6.3 %all-to-all-start.1 = ((bf16[4,1,4]{2,1,0:T(2,128)(2,1)}), bf16[4,1,4]{2,1,0:T(2,128)(2,1)S(1)}, u32[]{:S(2)}, u32[]{:S(2)}) async-start(bf16[4,1,4]{2,1,0:T(2,128)(2,1)} %convert_element_type.76), calls=%async_computation.1 | async-start | bytes 4096 | tf_op jit(solution)/shard_map/all_to_all | solution.py:95
  9.4 2.1 %fusion.137 = (f32[1]{0:T(128)}, f32[1]{0:T(128)}, f32[1]{0:T(128)}, f32[1]{0:T(128)}, f32[1]{0:T(128)}, /*index=5*/f32[1]{0:T(128)}, f32[1]{0:T(128)}, f32[1]{0...) fusion(f32[32]{0:T(128)} %param.8), kind=kLoop, calls=%fused_computation.186 | loop fusion | bytes 152 | tf_op jit(solution)/shard_map/slice | solution.py:29
  11.5 1.8 %fusion.138 = (f32[1]{0:T(128)}, f32[1]{0:T(128)}, f32[1]{0:T(128)}, f32[1]{0:T(128)}, f32[1]{0:T(128)}, /*index=5*/f32[1]{0:T(128)}, f32[1]{0:T(128)}, f32[1]{0...) fusion(f32[32]{0:T(128)} %param.8), kind=kLoop, calls=%fused_computation.187 | loop fusion | bytes 104 | tf_op jit(solution)/shard_map/slice | solution.py:29
  13.3 3.2 %pad_slice_fusion.1 = (bf16[16,8,12288]{2,1,0:T(8,128)(2,1)S(1)}, bf16[16,8,12288]{2,1,0:T(8,128)(2,1)S(1)}) fusion(bf16[16,8,12000]{2,1,0:T(8,128)(2,1)} %bitcast.115), kind=kLoop, calls=%fused_computation.6 | loop fusion | bytes 9363456 | tf_op jit(solution)/shard_map/slice | solution.py:21
  16.5 1.3 %copy.29 = bf16[16,8,24,512]{3,2,1,0:T(8,128)(2,1)S(1)} copy(bf16[16,8,24,512]{3,1,2,0:T(8,128)(2,1)S(1)} %bitcast.112) | data formatting | bytes 6291456
  17.8 0.1 slice.157
  17.9 1.3 %copy.30 = bf16[16,8,24,512]{3,2,1,0:T(8,128)(2,1)S(1)} copy(bf16[16,8,24,512]{3,1,2,0:T(8,128)(2,1)S(1)} %bitcast.111) | data formatting | bytes 6291456
  19.2 22.2 %fusion = f32[16,8,24,128]{3,2,1,0:T(8,128)S(1)} fusion(bf16[16,8,24,28]{3,2,1,0:T(8,128)(2,1)S(1)} %slice.157, bf16[16,8,24,512]{3,2,1,0:T(8,128)(2,1)S(1)} %copy.30, f32[]{:T(128)} %bitcast.35, f32[]{:T(128)} %bitcast.34, f32[]{:T(128)} %bitcast.33, f32[]{:T(128)} %bitcast.32, f32[]{:T(128)} %bitcast.31, f32[]{:T(128)} %bitcast.30, f32[]{:T(128)} %bitcast.29, ...), kind=kOutput, calls=%fused_computation.7 | convolution fusion | flops 438220800 | bytes 4891264 | tf_op jit(solution)/shard_map/iqbw,wn->iqbn/dot_general | solution.py:33
  41.4 22.0 %add_convert_fusion = bf16[16,8,24,128]{3,2,1,0:T(8,128)(2,1)S(1)} fusion(f32[16,8,24,128]{3,2,1,0:T(8,128)S(1)} %fusion, bf16[16,8,24,28]{3,2,1,0:T(8,128)(2,1)S(1)} %slice.157, bf16[16,8,24,512]{3,2,1,0:T(8,128)(2,1)S(1)} %copy.30, f32[]{:T(128)} %bitcast.35, f32[]{:T(128)} %bitcast.34, f32[]{:T(128)} %bitcast.33, f32[]{:T(128)} %bitcast.32, ...), kind=kOutput, calls=%fused_computation.11 | convolution fusion | flops 438799872 | bytes 5677696 | tf_op jit(solution)/shard_map/iqbw,wn->iqbn/dot_general | solution.py:32
  63.4 0.3 reshape.222
  63.8 3.6 %cosine_convert_fusion = (bf16[3000,64]{0,1:T(8,128)(2,1)S(1)}, bf16[3000,64]{0,1:T(8,128)(2,1)S(1)}) fusion(s32[64]{0:T(128)S(1)} %copy-done), kind=kLoop, calls=%fused_computation.21 | loop fusion | flops 2304000 | bytes 768256 | tf_op jit(solution)/shard_map/convert.1
  67.4 0.5 multiply_reduce_fusion
  68.0 0.6 gather_fusion
  68.6 0.7 broadcast_select_fusion
  69.3 5.1 %all-to-all-start = ((bf16[4,4,8,128]{3,2,1,0:T(8,128)(2,1)}), bf16[4,4,8,128]{3,2,1,0:T(8,128)(2,1)S(1)}, u32[]{:S(2)}, u32[]{:S(2)}) async-start(bf16[4,4,8,128]{3,2,1,0:T(8,128)(2,1)} %broadcast_select_fusion), calls=%async_computation | async-start | bytes 65536 | tf_op jit(solution)/shard_map/all_to_all | solution.py:94
  74.7 5.4 %all-to-all-done = bf16[4,4,8,128]{3,2,1,0:T(8,128)(2,1)S(1)} async-done(((bf16[4,4,8,128]{3,2,1,0:T(8,128)(2,1)}), bf16[4,4,8,128]{3,2,1,0:T(8,128)(2,1)S(1)}, u32[]{:S(2)}, u32[]{:S(2)}) %all-to-all-start) | async-done | bytes 32800 | tf_op jit(solution)/shard_map/all_to_all | solution.py:94
  80.1 0.6 gather_fusion.1
  80.6 13.3 %all-gather = bf16[64,8,128]{2,1,0:T(8,128)(2,1)S(1)} all-gather(bf16[16,8,128]{2,1,0:T(8,128)(2,1)S(1)} %gather_fusion.1), channel_id=2, replica_groups=mesh['groups'=2,'row'=4,'col'=4] {'row'}, dimensions={0}, use_global_device_ids=true | all-gather | bytes 163840 | tf_op jit(solution)/shard_map/all_gather | solution.py:107
  94.0 5.6 %all-gather.1 = bf16[64,8,128]{2,1,0:T(8,128)(2,1)S(1)} all-gather(bf16[16,8,128]{2,1,0:T(8,128)(2,1)S(1)} %gather_fusion.1), channel_id=3, replica_groups=mesh['groups'=2,'row'=4,'col'=4] {'col'}, dimensions={0}, use_global_device_ids=true | all-gather | bytes 163840 | tf_op jit(solution)/shard_map/all_gather | solution.py:100
  99.6 0.2 copy.19
  99.8 0.1 reshape.226
  100.0 0.4 copy.20
  100.4 0.5 fusion.44
  100.8 3.1 %copy.21 = f32[64,64,64]{0,1,2:T(8,128)} copy(f32[64,64,64]{2,1,0:T(8,128)S(1)} %fusion.44) | data formatting | bytes 2097152 | tf_op jit(solution)/shard_map/ikb,jkb->ijb/dot_general | solution.py:114
  103.9 0.5 fusion.48
  104.4 3.1 %copy.22 = f32[64,64,64]{0,1,2:T(8,128)} copy(f32[64,64,64]{2,1,0:T(8,128)S(1)} %fusion.48) | data formatting | bytes 2097152 | tf_op jit(solution)/shard_map/ikb,jkb->ijb/dot_general | solution.py:115
  107.5 3.8 %fusion.2 = bf16[64,1,64,128]{3,2,1,0:T(8,128)(2,1)} fusion(f32[64,1,64,64]{3,2,1,0:T(8,128)} %bitcast.114, f32[64,1,64,64]{3,2,1,0:T(8,128)} %bitcast.113), kind=kLoop, calls=%fused_computation.10 | loop fusion | flops 1572864 | bytes 3145728 | tf_op jit(solution)/shard_map/convert_element_type | solution.py:116
  (20 shorter events, 0.5 us)
Async XLA Ops:
  3.0 66.3 %all-to-all-start.1 = ((bf16[4,1,4]{2,1,0:T(2,128)(2,1)}), bf16[4,1,4]{2,1,0:T(2,128)(2,1)S(1)}, u32[]{:S(2)}, u32[]{:S(2)}) async-start(bf16[4,1,4]{2,1,0:T(2,128)(2,1)} %convert_element_type.76), calls=%async_computation.1 | async-start | bytes 4096 | tf_op jit(solution)/shard_map/all_to_all | solution.py:95
  41.4 22.4 %copy-start = (s32[64]{0:T(128)S(1)}, s32[64]{0:T(128)}, u32[]{:S(2)}) copy-start(s32[64]{0:T(128)} %param.9) | copy-start | bytes 772
  69.3 10.8 %all-to-all-start = ((bf16[4,4,8,128]{3,2,1,0:T(8,128)(2,1)}), bf16[4,4,8,128]{3,2,1,0:T(8,128)(2,1)S(1)}, u32[]{:S(2)}, u32[]{:S(2)}) async-start(bf16[4,4,8,128]{3,2,1,0:T(8,128)(2,1)} %broadcast_select_fusion), calls=%async_computation | async-start | bytes 65536 | tf_op jit(solution)/shard_map/all_to_all | solution.py:94
where the time goes:
time: 112 us; the launch traced here: 111 us
  matrix products  45.6 us (41%)
  local copies, waits for them, and re-layouts  19 us (17%)
  blocking collectives  18.9 us (17%)
  starting transfers between devices  11.4 us (10%)
  other arithmetic  10.1 us (9%)
  waiting for transfers between devices  5.41 us (5%)
    dot_general x1, matrix products, decimate(): jnp.einsum('iqbw,wn->iqbn', window, lower, preferred_element_type=jnp.flo...  22.2 us
    dot_general x1, matrix products, decimate(): jnp.einsum('iqbw,wn->iqbn', window, upper, preferred_element_type=jnp.flo...  22 us
    all_gather x1, blocking collectives, on_device(): piece = lax.all_gather(white_own, 'row', axis=0, tiled=True)  13.3 us
    all_to_all x1, starting transfers between devices, on_device(): lax.all_to_all(labels, 'row', split_axis=0, concat_axis=0, tiled=True)  6.35 us
    all_gather x1, blocking collectives, on_device(): row_white = lax.all_gather(white_own, 'col', axis=0, tiled=True)  5.58 us
    all_to_all x1, waiting for transfers between devices, on_device(): lax.all_to_all(outgoing, 'row', split_axis=0, concat_axis=0, tiled=True)  5.41 us
    all_to_all x1, starting transfers between devices, on_device(): lax.all_to_all(outgoing, 'row', split_axis=0, concat_axis=0, tiled=True)  5.09 us
    slice x2, local copies, waits for them, and re-layouts, decimate(): fir_taps[index]  3.9 us
  transfers between devices with their start and end apart: 2, of which 1 were waited for; matrix products, arithmetic and copies ran while one was open for 54% of the time, Pallas kernels for 0%

commit v1 on v0

v1 whole, which is shorter than its diff:
```python
import functools
import math

import jax
import jax.numpy as jnp
from jax import lax
from jax.experimental import pallas as pl
from jax.experimental.pallas import tpu as pltpu
from jax.sharding import PartitionSpec as P

CH_DEV = 16
DEC = 4
SPAN = 512
LANES = 128
TILE = 16
SIN = (6.283185307, -41.341702147, 81.60523051, -76.704495669, 42.014104466, -14.423992009)


def split(x):
    high = x.astype(jnp.bfloat16)
    return high, (x - high.astype(jnp.float32)).astype(jnp.bfloat16)


def turn_cos(steps, length):
    steps = steps - jnp.round(steps * (1.0 / length)) * length
    gap = 0.25 - jnp.abs(steps * (1.0 / length))
    square = gap * gap
    value = jnp.full_like(gap, SIN[-1])
    for term in SIN[-2::-1]:
        value = value * square + term
    return value * gap


def dot(a, b):
    return jnp.dot(a, b, preferred_element_type=jnp.float32)


def dot_t(a, b):
    return lax.dot_general(a, b, (((1,), (1,)), ((), ())), preferred_element_type=jnp.float32)


def iota(shape, axis):
    return lax.broadcasted_iota(jnp.int32, shape, axis)


def whiten_kernel(ncols, records, taps_count, counts, raw, taps, bins, channels, out, held, sems):
    rows, samples = raw.shape
    length = samples // DEC
    chunk = rows // sems.shape[0]
    copies = []
    for index in range(sems.shape[0]):
        part = pl.ds(index * chunk, chunk)
        copies.append(pltpu.make_async_copy(raw.at[part, :], held.at[part, :], sems.at[index]))
        copies[-1].start()
    width = out.shape[1]
    half = width // 2
    before = taps_count // DEC - 1
    depth = SPAN // DEC + before
    depth = (depth + TILE - 1) // TILE * TILE
    base = bins[...].astype(jnp.float32)
    band = jnp.concatenate([base, base], axis=1)
    quarter = jnp.where(iota((1, width), 1) < half, 0.0, 0.25 * length)
    eye = iota((width, width), 0) == iota((width, width), 1)
    band_col = jnp.sum(jnp.where(eye, band, 0.0), axis=1, keepdims=True)
    quarter_col = jnp.where(iota((width, 1), 0) < half, 0.0, 0.25 * length)
    place = iota((width, depth), 1)
    wave = turn_cos(band_col * (place - before).astype(jnp.float32) - quarter_col, length)
    wave_high, wave_low = split(wave)
    gap = iota((depth, SPAN), 1) - DEC * (iota((depth, SPAN), 0) - before)
    lane_taps = jnp.concatenate([taps[...], jnp.zeros((1, LANES - taps_count), jnp.float32)], axis=1)
    lane_taps = jnp.broadcast_to(lane_taps, (depth, LANES))
    pieces = []
    for start in range(0, SPAN, LANES):
        where = gap[:, start : start + LANES]
        found = jnp.take_along_axis(lane_taps, jnp.clip(where, 0, taps_count - 1), axis=1)
        pieces.append(jnp.where((where >= 0) & (where < taps_count), found, 0.0))
    banded = jnp.concatenate(pieces, axis=1)
    band_high, band_low = split(banded)
    table = dot(wave_high, band_high) + dot(wave_high, band_low) + dot(wave_low, band_high)
    table = jnp.concatenate(split(table), axis=0)
    early = place < before
    early_high = jnp.where(early, wave_high.astype(jnp.float32), 0.0).astype(jnp.bfloat16)
    early_low = jnp.where(early, wave_low.astype(jnp.float32), 0.0).astype(jnp.bfloat16)
    first_high, first_low = band_high[:, :LANES], band_low[:, :LANES]
    edge = dot(early_high, first_high) + dot(early_high, first_low) + dot(early_low, first_high)
    edge = jnp.concatenate(split(edge), axis=0)
    blocks = (samples + SPAN - 1) // SPAN
    turns = (iota((blocks, width), 0) * (SPAN // DEC)).astype(jnp.float32) * band
    cosine = turn_cos(turns, length)
    sine = turn_cos(turns - 0.25 * length, length)
    sign = jnp.where(iota((1, width), 1) < half, 1.0, -1.0)
    slots = rows // records
    for index in range(sems.shape[0]):
        copies[index].wait()
        part = pl.ds(index * chunk, chunk)
        along = jnp.zeros((chunk, width), jnp.float32)
        across = jnp.zeros((chunk, width), jnp.float32)
        for block in range(blocks):
            size = min(SPAN, samples - block * SPAN)
            piece = held[part, block * SPAN : block * SPAN + size]
            both = dot_t(piece, table[:, :size])
            term = both[:, :width] + both[:, width:]
            if block == 0:
                fix = dot_t(piece[:, :LANES], edge)
                along = term - fix[:, :width] - fix[:, width:]
            else:
                along = along + term * cosine[block : block + 1]
                across = across + term * sine[block : block + 1]
        spectra = along * sign - pltpu.roll(across, half, 1)
        power = jnp.mean(spectra * spectra, axis=1, keepdims=True)
        white = spectra / jnp.sqrt(power + 1e-06)
        slot = (iota((chunk, 1), 0) + index * chunk) // records
        out[part, :] = jnp.where(slot < counts[0, 0], white, 0.0).astype(out.dtype)
    owner = channels[...] // (CH_DEV * ncols)
    local = owner * CH_DEV + channels[...] % CH_DEV
    local = jnp.where(iota((1, slots), 1) < counts[0, 0], local, -1).astype(jnp.float32)
    local = jnp.broadcast_to(
        jnp.concatenate([local, jnp.zeros((1, LANES - slots), jnp.float32)], axis=1), (TILE, LANES)
    )
    source = iota((TILE, LANES), 0) * (LANES // records) + iota((TILE, LANES), 1) // records
    labels = jnp.take_along_axis(local, jnp.minimum(source, slots - 1), axis=1)
    out[rows:, :] = labels.astype(out.dtype)


def whiten(raw_files, file_channels, reader_counts, fir_taps, band_bins, ncols):
    slots, _, records, samples = raw_files.shape
    rows = slots * records
    width = 2 * band_bins.shape[0]
    chunks = 2
    vmem = pl.BlockSpec(memory_space=pltpu.VMEM)
    return pl.pallas_call(
        functools.partial(whiten_kernel, ncols, records, fir_taps.shape[0]),
        out_shape=jax.ShapeDtypeStruct((rows + TILE, width), jnp.bfloat16),
        in_specs=[
            pl.BlockSpec(memory_space=pltpu.SMEM),
            pl.BlockSpec(memory_space=pl.ANY),
            vmem,
            vmem,
            vmem,
        ],
        out_specs=vmem,
        scratch_shapes=[pltpu.VMEM((rows, samples), jnp.bfloat16), pltpu.SemaphoreType.DMA((chunks,))],
        name="whiten",
    )(
        reader_counts,
        raw_files.reshape(rows, samples),
        fir_taps.reshape(1, -1),
        band_bins.reshape(1, -1),
        file_channels.reshape(1, -1),
    )


def placing(packet, targets, records):
    rows = packet.shape[0] - TILE
    picks = []
    for group in range(rows // LANES):
        labels = packet[rows : rows + TILE, :].astype(jnp.float32)[group : group + 1]
        keys = labels * records + (iota((1, LANES), 1) % records).astype(jnp.float32)
        picks.append((targets == keys).astype(jnp.float32).astype(jnp.bfloat16))
    return jnp.concatenate(picks, axis=1)


def gather_rows(packets, targets, records):
    picks = jnp.concatenate([placing(p, targets, records) for p in packets], axis=1)
    data = jnp.concatenate([p[: p.shape[0] - TILE, :] for p in packets], axis=0)
    return dot(picks, data)


def own_kernel(records, *refs):
    packets, out = refs[:-1], refs[-1]
    count = out.shape[0]
    first = lax.axis_index("row") * count
    targets = (iota((count, 1), 0) + first).astype(jnp.float32)
    out[...] = gather_rows(packets, targets, records).astype(out.dtype)


def own_block(packets, records):
    vmem = pl.BlockSpec(memory_space=pltpu.VMEM)
    return pl.pallas_call(
        functools.partial(own_kernel, records),
        out_shape=jax.ShapeDtypeStruct((CH_DEV * records, packets[0].shape[1]), packets[0].dtype),
        in_specs=[vmem] * len(packets),
        out_specs=vmem,
        name="own",
    )(*packets)


def stack_kernel(records, nrows, ncols, *refs):
    packets = refs[:nrows]
    lefts = refs[nrows : nrows + ncols]
    out, right_re, right_im, left, left_turned, tiles, sems = refs[nrows + ncols :]
    width = out.shape[2]
    half = width // 2
    count = nrows * CH_DEV
    low = iota((1, width), 1) < half
    for start in range(0, count, 64):
        block = min(64, count - start)
        for record in range(records):
            targets = ((iota((block, 1), 0) + start) * records + record).astype(jnp.float32)
            placed = gather_rows(packets, targets, records)
            swapped = pltpu.roll(placed, half, 1)
            right_re[record, start : start + block, :] = jnp.where(low, placed, swapped)
            right_im[record, start : start + block, :] = jnp.where(low, swapped, placed)
    mine = lax.axis_index("col")
    scale = 1.0 / records
    copies = []
    for step in range(ncols):
        piece = lefts[step][...].astype(jnp.float32) * scale
        swapped = pltpu.roll(piece, half, 1)
        left_turned[...] = jnp.where(low, swapped, -swapped)
        left[...] = piece

        @pl.loop(0, count // TILE)
        def _(j):
            rows = pl.ds(pl.multiple_of(j * TILE, TILE), TILE)
            res = [right_re[e, rows, :] for e in range(records)]
            ims = [right_im[e, rows, :] for e in range(records)]
            for k in range(CH_DEV):
                total = None
                for e in range(records):
                    a = left[k * records + e : k * records + e + 1, :]
                    b = left_turned[k * records + e : k * records + e + 1, :]
                    term = a * res[e] + b * ims[e]
                    total = term if total is None else total + term
                tiles[step, k, rows, :] = total.astype(tiles.dtype)

        place = lax.rem(mine - step + ncols, ncols)
        copies.append(
            pltpu.make_async_copy(tiles.at[step], out.at[pl.ds(place * CH_DEV, CH_DEV)], sems.at[step])
        )
        copies[-1].start()
    for copy in copies:
        copy.wait()


def stacked(packets, lefts, records):
    nrows, ncols = len(packets), len(lefts)
    width = packets[0].shape[1]
    count = nrows * CH_DEV
    vmem = pl.BlockSpec(memory_space=pltpu.VMEM)
    return pl.pallas_call(
        functools.partial(stack_kernel, records, nrows, ncols),
        out_shape=jax.ShapeDtypeStruct((ncols * CH_DEV, count, width), jnp.bfloat16),
        in_specs=[vmem] * (nrows + ncols),
        out_specs=pl.BlockSpec(memory_space=pl.ANY),
        scratch_shapes=[
            pltpu.VMEM((records, count, width), jnp.float32),
            pltpu.VMEM((records, count, width), jnp.float32),
            pltpu.VMEM((CH_DEV * records, width), jnp.float32),
            pltpu.VMEM((CH_DEV * records, width), jnp.float32),
            pltpu.VMEM((ncols, CH_DEV, count, width), jnp.bfloat16),
            pltpu.SemaphoreType.DMA((ncols,)),
        ],
        name="stack",
    )(*packets, *lefts)


def shifted(block, axis):
    size = lax.axis_size(axis)
    return [block] + [
        lax.ppermute(block, axis, [(i, (i + s) % size) for i in range(size)]) for s in range(1, size)
    ]


def on_device(raw_files, file_channels, reader_counts, fir_taps, band_bins):
    ncols = lax.axis_size("col")
    records = raw_files.shape[2]
    packet = whiten(raw_files, file_channels, reader_counts, fir_taps, band_bins, ncols)
    packets = shifted(packet, "row")
    own = own_block(packets, records)
    lefts = shifted(own, "col")
    return stacked(packets, lefts, records)[:, None, :, :]


def solution(mesh):
    return jax.shard_map(
        on_device,
        mesh=mesh,
        in_specs=(
            P(("groups", "row"), "col", None, None),
            P(("groups", "row"), "col"),
            P(("groups", "row"), "col"),
            P(),
            P(),
        ),
        out_specs=P(("groups", "row"), "col", None, None),
        check_vma=False,
    )
```

time: 112 us -> 31.3 us (0.28)
  matrix products: 45.6 us -> 0 us
  blocking collectives: 18.9 us -> 0 us
  local copies, waits for them, and re-layouts: 19 us -> 1.23 us
  Pallas kernels: 0 us -> 12.9 us
  other arithmetic: 10.1 us -> 0 us
  starting transfers between devices: 11.4 us -> 7.86 us
  waiting for transfers between devices: 5.41 us -> 8.27 us
    dot_general x5 -> x0, matrix products: 45.6 us -> none  [the longest x1 22.2 us: decimate(): jnp.einsum('iqbw,wn->iqbn', window, lower, preferred_element_type=jnp.flo...]
    all_gather x2 -> x0, blocking collectives: 18.9 us -> none  [the longest x1 13.3 us: on_device(): piece = lax.all_gather(white_own, 'row', axis=0, tiled=True)]
    pallas_call x0 -> x3, Pallas kernels: none -> 12.9 us  [the longest x1 6.77 us: whiten(): pl.pallas_call(functools.partial(whiten_kernel, ncols, records, fir_taps....]
    all_to_all x2 -> x0, starting transfers between devices: 11.4 us -> none  [the longest x1 6.35 us: on_device(): lax.all_to_all(labels, 'row', split_axis=0, concat_axis=0, tiled=True)]
    ppermute x0 -> x6, waiting for transfers between devices: none -> 8.27 us  [shifted(): lax.ppermute(block, axis, [(i, (i + s) % size) for i in range(size)])]
    ppermute x0 -> x6, starting transfers between devices: none -> 7.86 us  [shifted(): lax.ppermute(block, axis, [(i, (i + s) % size) for i in range(size)])]
    slice x4 -> x0, local copies, waits for them, and re-layouts: 7.24 us -> none  [the longest x2 3.9 us: decimate(): fir_taps[index]]
    dot_general x2 -> x0, local copies, waits for them, and re-layouts: 6.14 us -> none  [the longest x1 3.07 us: on_device(): jnp.einsum('ikb,jkb->ijb', left, right_real, preferred_element_type=jnp.f...]
  transfers between devices with their start and end apart: 2 -> 6, of which waited for: 1 -> 6; matrix products, arithmetic and copies ran while one was open for 54% -> 0% of each run, Pallas kernels for 0% -> 0%
where the time goes in v1:
time: 31.3 us; the launch traced here: 31 us
  Pallas kernels  12.9 us (41%)
  waiting for transfers between devices  8.27 us (26%)
  starting transfers between devices  7.86 us (25%)
  local copies, waits for them, and re-layouts  1.23 us (4%)
  between operations  0.67 us (2%)
    ppermute x6, waiting for transfers between devices, shifted(): lax.ppermute(block, axis, [(i, (i + s) % size) for i in range(size)])  8.27 us
    ppermute x6, starting transfers between devices, shifted(): lax.ppermute(block, axis, [(i, (i + s) % size) for i in range(size)])  7.86 us
    pallas_call x1, Pallas kernels, whiten(): pl.pallas_call(functools.partial(whiten_kernel, ncols, records, fir_taps....  6.77 us
    pallas_call x1, Pallas kernels, stacked(): pl.pallas_call(functools.partial(stack_kernel, records, nrows, ncols), ou...  4.56 us
    pallas_call x1, Pallas kernels, own_block(): pl.pallas_call(functools.partial(own_kernel, records), out_shape=jax.Shap...  1.6 us
    unnamed x12, local copies, waits for them, and re-layouts  1.23 us
  transfers between devices with their start and end apart: 6, of which 6 were waited for; matrix products, arithmetic and copies ran while one was open for 0% of the time, Pallas kernels for 0%

profile of v1, /device:TPU:0, one launch (start us, length us, event | category | flops | bytes accessed | tf_op | source)
XLA Modules:
  0.0 31.0 jit_solution(16191377137968866950)
XLA Ops:
  0.7 6.8 %whiten.1.refs_0_ = bf16[144,128]{1,0:T(8,128)(2,1)} custom-call(s32[1,1]{1,0:T(1,128)S(6)} %copy.7.counts, bf16[128,12000]{1,0:T(8,128)(2,1)} %bitcast.7, f32[1,32]{1,0:T(1,128)} %bitcast.8, s32[1,64]{1,0:T(1,128)} %bitcast.9, s32[1,16]{1,0:T(1,128)} %bitcast.10), custom_call_target="tpu_custom_call" | custom-call | tf_op jit(solution)/shard_map/whiten/pallas_call | solution.py:131
  7.4 5.1 %collective-permute-start.2 = (bf16[144,128]{1,0:T(8,128)(2,1)}, bf16[144,128]{1,0:T(8,128)(2,1)S(1)}, u32[]{:S(2)}, u32[]{:S(2)}) collective-permute-start(bf16[144,128]{1,0:T(8,128)(2,1)} %whiten.1.refs_0_), channel_id=1, source_target_pairs={{0,12},{4,0},{8,4},{12,8},{1,13},{5,1},{9,5},{13,9},{2,14},{6,2},{... | collective-permute-start | bytes 110600 | tf_op jit(solution)/shard_map/ppermute | solution.py:261
  12.6 0.0 collective-permute-start.1
  12.6 1.0 %collective-permute-start = (bf16[144,128]{1,0:T(8,128)(2,1)}, bf16[144,128]{1,0:T(8,128)(2,1)S(1)}, u32[]{:S(2)}, u32[]{:S(2)}) collective-permute-start(bf16[144,128]{1,0:T(8,128)(2,1)} %whiten.1.refs_0_), channel_id=1, source_target_pairs={{0,4},{4,8},{8,12},{12,0},{1,5},{5,9},{9,13},{13,1},{2,6},{6,10},{... | collective-permute-start | bytes 110600 | tf_op jit(solution)/shard_map/ppermute | solution.py:261
  13.6 0.9 %collective-permute-done.2.refs_3_ = bf16[144,128]{1,0:T(8,128)(2,1)S(1)} collective-permute-done((bf16[144,128]{1,0:T(8,128)(2,1)}, bf16[144,128]{1,0:T(8,128)(2,1)S(1)}, u32[]{:S(2)}, u32[]{:S(2)}) %collective-permute-start.2) | collective-permute-done | bytes 36896 | tf_op jit(solution)/shard_map/ppermute | solution.py:261
  14.5 0.0 copy-start
  14.5 3.1 %collective-permute-done.1.refs_2_ = bf16[144,128]{1,0:T(8,128)(2,1)S(1)} collective-permute-done((bf16[144,128]{1,0:T(8,128)(2,1)}, bf16[144,128]{1,0:T(8,128)(2,1)S(1)}, u32[]{:S(2)}, u32[]{:S(2)}) %collective-permute-start.1) | collective-permute-done | bytes 36896 | tf_op jit(solution)/shard_map/ppermute | solution.py:261
  17.6 0.0 copy-start.1
  17.6 0.9 %collective-permute-done.refs_1_ = bf16[144,128]{1,0:T(8,128)(2,1)S(1)} collective-permute-done((bf16[144,128]{1,0:T(8,128)(2,1)}, bf16[144,128]{1,0:T(8,128)(2,1)S(1)}, u32[]{:S(2)}, u32[]{:S(2)}) %collective-permute-start) | collective-permute-done | bytes 36896 | tf_op jit(solution)/shard_map/ppermute | solution.py:261
  18.5 0.0 copy-done
  18.5 0.0 copy-done.1
  18.5 0.0 copy-start.2
  18.5 0.6 %copy-done.2 = bf16[144,128]{1,0:T(8,128)(2,1)} copy-done((bf16[144,128]{1,0:T(8,128)(2,1)}, bf16[144,128]{1,0:T(8,128)(2,1)S(1)}, u32[]{:S(2)}) %copy-start.2) | copy-done | bytes 36888
  19.2 1.6 %own.1.refs_4_ = bf16[128,128]{1,0:T(8,128)(2,1)} custom-call(bf16[144,128]{1,0:T(8,128)(2,1)} %whiten.1.refs_0_, bf16[144,128]{1,0:T(8,128)(2,1)} %copy-done.2, bf16[144,128]{1,0:T(8,128)(2,1)} %copy-done.1, bf16[144,128]{1,0:T(8,128)(2,1)} %copy-done), custom_call_target="tpu_custom_call" | custom-call | tf_op jit(solution)/shard_map/own/pallas_call | solution.py:179
  20.8 0.0 collective-permute-start.5
  20.8 1.5 %collective-permute-start.4 = (bf16[128,128]{1,0:T(8,128)(2,1)}, bf16[128,128]{1,0:T(8,128)(2,1)S(1)}, u32[]{:S(2)}, u32[]{:S(2)}) collective-permute-start(bf16[128,128]{1,0:T(8,128)(2,1)} %own.1.refs_4_), channel_id=1, source_target_pairs={{0,2},{1,3},{2,0},{3,1},{4,6},{5,7},{6,4},{7,5},{8,10},{9,11},{10,... | collective-permute-start | bytes 98312 | tf_op jit(solution)/shard_map/ppermute | solution.py:261
  22.2 0.2 collective-permute-start.3
  22.5 0.2 collective-permute-done.5.refs_7_
  22.7 0.0 copy-start.3
  22.7 2.4 %collective-permute-done.4.refs_6_ = bf16[128,128]{1,0:T(8,128)(2,1)S(1)} collective-permute-done((bf16[128,128]{1,0:T(8,128)(2,1)}, bf16[128,128]{1,0:T(8,128)(2,1)S(1)}, u32[]{:S(2)}, u32[]{:S(2)}) %collective-permute-start.4) | collective-permute-done | bytes 32800 | tf_op jit(solution)/shard_map/ppermute | solution.py:261
  25.0 0.0 copy-start.4
  25.0 0.7 %collective-permute-done.3.refs_5_ = bf16[128,128]{1,0:T(8,128)(2,1)S(1)} collective-permute-done((bf16[128,128]{1,0:T(8,128)(2,1)}, bf16[128,128]{1,0:T(8,128)(2,1)S(1)}, u32[]{:S(2)}, u32[]{:S(2)}) %collective-permute-start.3) | collective-permute-done | bytes 32800 | tf_op jit(solution)/shard_map/ppermute | solution.py:261
  25.8 0.0 copy-done.3
  25.8 0.0 copy-done.4
  25.8 0.0 copy-start.5
  25.8 0.6 %copy-done.5 = bf16[128,128]{1,0:T(8,128)(2,1)} copy-done((bf16[128,128]{1,0:T(8,128)(2,1)}, bf16[128,128]{1,0:T(8,128)(2,1)S(1)}, u32[]{:S(2)}) %copy-start.5) | copy-done | bytes 32792
  26.4 4.6 %stack.1 = bf16[64,64,128]{2,1,0:T(8,128)(2,1)} custom-call(bf16[144,128]{1,0:T(8,128)(2,1)} %whiten.1.refs_0_, bf16[144,128]{1,0:T(8,128)(2,1)} %copy-done.2, bf16[144,128]{1,0:T(8,128)(2,1)} %copy-done.1, bf16[144,128]{1,0:T(8,128)(2,1)} %copy-done, bf16[128,128]{1,0:T(8,128)(2,1)} %own.1.refs_4_, bf16[128,128]{1,0:T(8,128)(2,1)} %copy-done.5, ...), custom_call_target="tpu_custom_call" | custom-call | tf_op jit(solution)/shard_map/stack/pallas_call | solution.py:241
Async XLA Ops:
  7.4 7.1 %collective-permute-start.2 = (bf16[144,128]{1,0:T(8,128)(2,1)}, bf16[144,128]{1,0:T(8,128)(2,1)S(1)}, u32[]{:S(2)}, u32[]{:S(2)}) collective-permute-start(bf16[144,128]{1,0:T(8,128)(2,1)} %whiten.1.refs_0_), channel_id=1, source_target_pairs={{0,12},{4,0},{8,4},{12,8},{1,13},{5,1},{9,5},{13,9},{2,14},{6,2},{... | collective-permute-start | bytes 110600 | tf_op jit(solution)/shard_map/ppermute | solution.py:261
  12.6 5.1 %collective-permute-start.1 = (bf16[144,128]{1,0:T(8,128)(2,1)}, bf16[144,128]{1,0:T(8,128)(2,1)S(1)}, u32[]{:S(2)}, u32[]{:S(2)}) collective-permute-start(bf16[144,128]{1,0:T(8,128)(2,1)} %whiten.1.refs_0_), channel_id=1, source_target_pairs={{0,8},{4,12},{8,0},{12,4},{1,9},{5,13},{9,1},{13,5},{2,10},{6,14},... | collective-permute-start | bytes 110600 | tf_op jit(solution)/shard_map/ppermute | solution.py:261
  12.6 6.0 %collective-permute-start = (bf16[144,128]{1,0:T(8,128)(2,1)}, bf16[144,128]{1,0:T(8,128)(2,1)S(1)}, u32[]{:S(2)}, u32[]{:S(2)}) collective-permute-start(bf16[144,128]{1,0:T(8,128)(2,1)} %whiten.1.refs_0_), channel_id=1, source_target_pairs={{0,4},{4,8},{8,12},{12,0},{1,5},{5,9},{9,13},{13,1},{2,6},{6,10},{... | collective-permute-start | bytes 110600 | tf_op jit(solution)/shard_map/ppermute | solution.py:261
  14.5 4.0 %copy-start = (bf16[144,128]{1,0:T(8,128)(2,1)}, bf16[144,128]{1,0:T(8,128)(2,1)S(1)}, u32[]{:S(2)}) copy-start(bf16[144,128]{1,0:T(8,128)(2,1)S(1)} %collective-permute-done.2.refs_3_) | copy-start | bytes 110596
  17.6 0.9 %copy-start.1 = (bf16[144,128]{1,0:T(8,128)(2,1)}, bf16[144,128]{1,0:T(8,128)(2,1)S(1)}, u32[]{:S(2)}) copy-start(bf16[144,128]{1,0:T(8,128)(2,1)S(1)} %collective-permute-done.1.refs_2_) | copy-start | bytes 110596
  18.5 0.6 %copy-start.2 = (bf16[144,128]{1,0:T(8,128)(2,1)}, bf16[144,128]{1,0:T(8,128)(2,1)S(1)}, u32[]{:S(2)}) copy-start(bf16[144,128]{1,0:T(8,128)(2,1)S(1)} %collective-permute-done.refs_1_) | copy-start | bytes 110596
  20.8 1.9 %collective-permute-start.5 = (bf16[128,128]{1,0:T(8,128)(2,1)}, bf16[128,128]{1,0:T(8,128)(2,1)S(1)}, u32[]{:S(2)}, u32[]{:S(2)}) collective-permute-start(bf16[128,128]{1,0:T(8,128)(2,1)} %own.1.refs_4_), channel_id=1, source_target_pairs={{0,3},{1,0},{2,1},{3,2},{4,7},{5,4},{6,5},{7,6},{8,11},{9,8},{10,9... | collective-permute-start | bytes 98312 | tf_op jit(solution)/shard_map/ppermute | solution.py:261
  20.8 4.3 %collective-permute-start.4 = (bf16[128,128]{1,0:T(8,128)(2,1)}, bf16[128,128]{1,0:T(8,128)(2,1)S(1)}, u32[]{:S(2)}, u32[]{:S(2)}) collective-permute-start(bf16[128,128]{1,0:T(8,128)(2,1)} %own.1.refs_4_), channel_id=1, source_target_pairs={{0,2},{1,3},{2,0},{3,1},{4,6},{5,7},{6,4},{7,5},{8,10},{9,11},{10,... | collective-permute-start | bytes 98312 | tf_op jit(solution)/shard_map/ppermute | solution.py:261
  22.2 3.6 %collective-permute-start.3 = (bf16[128,128]{1,0:T(8,128)(2,1)}, bf16[128,128]{1,0:T(8,128)(2,1)S(1)}, u32[]{:S(2)}, u32[]{:S(2)}) collective-permute-start(bf16[128,128]{1,0:T(8,128)(2,1)} %own.1.refs_4_), channel_id=1, source_target_pairs={{0,1},{1,2},{2,3},{3,0},{4,5},{5,6},{6,7},{7,4},{8,9},{9,10},{10,1... | collective-permute-start | bytes 98312 | tf_op jit(solution)/shard_map/ppermute | solution.py:261
  22.7 3.1 %copy-start.3 = (bf16[128,128]{1,0:T(8,128)(2,1)}, bf16[128,128]{1,0:T(8,128)(2,1)S(1)}, u32[]{:S(2)}) copy-start(bf16[128,128]{1,0:T(8,128)(2,1)S(1)} %collective-permute-done.5.refs_7_) | copy-start | bytes 98308
  25.0 0.8 %copy-start.4 = (bf16[128,128]{1,0:T(8,128)(2,1)}, bf16[128,128]{1,0:T(8,128)(2,1)S(1)}, u32[]{:S(2)}) copy-start(bf16[128,128]{1,0:T(8,128)(2,1)S(1)} %collective-permute-done.4.refs_6_) | copy-start | bytes 98308
  25.8 0.6 %copy-start.5 = (bf16[128,128]{1,0:T(8,128)(2,1)}, bf16[128,128]{1,0:T(8,128)(2,1)S(1)}, u32[]{:S(2)}) copy-start(bf16[128,128]{1,0:T(8,128)(2,1)S(1)} %collective-permute-done.3.refs_5_) | copy-start | bytes 98308

commit v2 on v1

v2 whole, which is shorter than its diff:
```python
import functools
import math

import jax
import jax.numpy as jnp
from jax import lax
from jax.experimental import pallas as pl
from jax.experimental.pallas import tpu as pltpu
from jax.sharding import PartitionSpec as P

CH_DEV = 16
DEC = 4
SPAN = 512
LANES = 128
TILE = 16
CHUNK = 64
BEHIND = 4
MXU = 256
SMALL = 16 << 20
ROW_ORDER = (1, 2, 3)
COL_ORDER = (1, 2, 3)
SIN = (6.283185307, -41.341702147, 81.60523051, -76.704495669, 42.014104466, -14.423992009)


def split(x):
    high = x.astype(jnp.bfloat16)
    return high, (x - high.astype(jnp.float32)).astype(jnp.bfloat16)


def turn_cos(steps, length):
    steps = steps - jnp.round(steps * (1.0 / length)) * length
    gap = 0.25 - jnp.abs(steps * (1.0 / length))
    square = gap * gap
    value = jnp.full_like(gap, SIN[-1])
    for term in SIN[-2::-1]:
        value = value * square + term
    return value * gap


def dot(a, b):
    return jnp.dot(a, b, preferred_element_type=jnp.float32)


def dot_t(a, b):
    return lax.dot_general(a, b, (((1,), (1,)), ((), ())), preferred_element_type=jnp.float32)


def iota(shape, axis):
    return lax.broadcasted_iota(jnp.int32, shape, axis)


def whiten_kernel(ncols, records, counts, raw, taps_in, bins_in, channels_in, out, held, taps, bins, channels, sems):
    rows, samples = raw.shape
    taps_count = taps.shape[1]
    length = samples // DEC
    chunks = rows // CHUNK
    small = []
    for index, (source, target) in enumerate(((taps_in, taps), (bins_in, bins), (channels_in, channels))):
        small.append(pltpu.make_async_copy(source, target, sems.at[chunks + index]))
        small[-1].start()
    copies = []
    for index in range(chunks):
        part = pl.ds(index * CHUNK, CHUNK)
        copies.append(pltpu.make_async_copy(raw.at[part, :], held.at[part, :], sems.at[index]))
        copies[-1].start()
    for copy in small:
        copy.wait()
    width = out.shape[1]
    half = width // 2
    before = taps_count // DEC - 1
    reach = LANES // DEC + before
    depth = (reach + TILE - 1) // TILE * TILE
    base = bins[...].astype(jnp.float32)
    band = jnp.concatenate([base, base], axis=1)
    eye = iota((width, width), 0) == iota((width, width), 1)
    band_col = jnp.sum(jnp.where(eye, band, 0.0), axis=1, keepdims=True)
    upper = iota((width, 1), 0) < half
    quarter = 0.25 * length
    place = iota((width, LANES), 1)
    extra = place - reach
    steps = jnp.where(place < reach, place - before, (extra // 2 + 1) * (LANES // DEC))
    shift = jnp.where(place < reach, iota((width, LANES), 0) // half, extra % 2)
    angles = band_col * steps.astype(jnp.float32) - shift.astype(jnp.float32) * quarter
    values = turn_cos(angles, length)
    wave = jnp.where(place < reach, values, 0.0)
    gap = iota((depth, LANES), 1) - DEC * (iota((depth, LANES), 0) - before)
    lane_taps = jnp.concatenate([taps[...], jnp.zeros((1, LANES - taps_count), jnp.float32)], axis=1)
    lane_taps = jnp.broadcast_to(lane_taps, (depth, LANES))
    banded = jnp.take_along_axis(lane_taps, jnp.clip(gap, 0, taps_count - 1), axis=1)
    band_high, band_low = split(jnp.where((gap >= 0) & (gap < taps_count), banded, 0.0))

    nothing = jnp.zeros((depth, LANES), jnp.bfloat16)
    gap_rows = jnp.zeros((LANES - depth, 2 * LANES), jnp.bfloat16)
    taps_rhs = jnp.concatenate(
        [
            jnp.concatenate([band_high, band_low], axis=1),
            gap_rows,
            jnp.concatenate([band_high, nothing], axis=1),
            gap_rows,
        ],
        axis=0,
    )
    waves = jnp.concatenate([wave, jnp.where(place < before, -wave, 0.0)], axis=0)
    waves = jnp.concatenate(split(waves), axis=1)

    def product(acc):
        pltpu.matmul_push_rhs(taps_rhs, 0, 0)
        pltpu.matmul_acc_lhs(acc, waves, load_staged_rhs=0)
        both = pltpu.matmul_pop(acc)
        return both[:, :LANES] + both[:, LANES:]

    filtered = pl.run_scoped(product, pltpu.ACC(0)((2 * width, MXU), jnp.float32))
    first, edge = filtered[:width], filtered[width:]
    swapped = jnp.concatenate([first[half:], first[:half]], axis=0)
    pieces = [first]
    for index in range(SPAN // LANES - 1):
        lane = reach + 2 * index
        cosine, sine = values[:, lane : lane + 1], values[:, lane + 1 : lane + 2]
        pieces.append(first * cosine + swapped * jnp.where(upper, -sine, sine))
    table = jnp.concatenate(split(jnp.concatenate(pieces, axis=1)), axis=0)
    edge = jnp.concatenate(split(edge), axis=0)
    edge = jnp.concatenate([edge, jnp.zeros((2 * width, MXU - LANES), jnp.bfloat16)], axis=1)
    blocks = (samples + SPAN - 1) // SPAN
    turns = (iota((blocks, width), 0) * (SPAN // DEC)).astype(jnp.float32) * band
    cosine = turn_cos(turns, length)
    sine = turn_cos(turns - quarter, length)
    sign = jnp.where(iota((1, width), 1) < half, 1.0, -1.0)
    slots = rows // records
    half_tables = [table[:, index * MXU : (index + 1) * MXU] for index in range(SPAN // MXU)]

    def piece(part, start):
        size = min(MXU, samples - start)
        block = held[part, start : start + size]
        if size < MXU:
            block = jnp.concatenate([block, jnp.zeros((CHUNK, MXU - size), block.dtype)], axis=1)
        return block

    per_unit = (blocks + 1) // 2
    accs = [pltpu.ACC(block % 2)((CHUNK, 2 * width), jnp.float32) for block in range(blocks)]

    def finish(index, along, across):
        spectra = along * sign - pltpu.roll(across, half, 1)
        power = jnp.mean(spectra * spectra, axis=1, keepdims=True)
        white = spectra / jnp.sqrt(power + 1e-06)
        slot = (iota((CHUNK, 1), 0) + index * CHUNK) // records
        out[index * CHUNK : (index + 1) * CHUNK, :] = jnp.where(slot < counts[0, 0], white, 0.0).astype(out.dtype)

    def every_chunk(*accs):
        along = across = None

        def pop(block, along, across):
            both = pltpu.matmul_pop(accs[block])
            term = both[:, :width] + both[:, width:]
            if block == 0:
                return term, jnp.zeros_like(term)
            return along + term * cosine[block : block + 1], across + term * sine[block : block + 1]

        for index in range(chunks):
            copies[index].wait()
            part = pl.ds(index * CHUNK, CHUNK)
            popped = 0
            for step in range(SPAN // MXU):
                for unit in range(2):
                    pltpu.matmul_push_rhs(half_tables[step], step, unit, transpose=True)
                fresh = [step, step]
                for block in range(blocks):
                    if step == 0 and index > 0:
                        along, across = pop(block, along, across)
                    start = block * SPAN + step * MXU
                    if start < samples:
                        if start == 0:
                            pltpu.matmul_push_rhs(edge, 1, 0, transpose=True)
                            pltpu.matmul_acc_lhs(accs[0], piece(part, 0), load_staged_rhs=1)
                        pltpu.matmul_acc_lhs(accs[block], piece(part, start), load_staged_rhs=fresh[block % 2])
                        fresh[block % 2] = None
                    if step == SPAN // MXU - 1 and index == chunks - 1 and block >= BEHIND:
                        along, across = pop(popped, along, across)
                        popped += 1
                if step == 0 and index > 0:
                    finish(index - 1, along, across)
                    along = across = None
        for block in range(popped, blocks):
            along, across = pop(block, along, across)
        finish(chunks - 1, along, across)

    pl.run_scoped(every_chunk, *accs)
    owner = channels[...] // (CH_DEV * ncols)
    local = owner * CH_DEV + channels[...] % CH_DEV
    local = jnp.where(iota((1, slots), 1) < counts[0, 0], local, -1).astype(jnp.float32)
    local = jnp.broadcast_to(
        jnp.concatenate([local, jnp.zeros((1, LANES - slots), jnp.float32)], axis=1), (TILE, LANES)
    )
    source = iota((TILE, LANES), 0) * (LANES // records) + iota((TILE, LANES), 1) // records
    labels = jnp.take_along_axis(local, jnp.minimum(source, slots - 1), axis=1)
    out[rows:, :] = labels.astype(out.dtype)


def whiten(raw_files, file_channels, reader_counts, fir_taps, band_bins, ncols):
    slots, _, records, samples = raw_files.shape
    rows = slots * records
    bins = band_bins.shape[0]
    taps = fir_taps.shape[0]
    width = 2 * bins
    anywhere = pl.BlockSpec(memory_space=pl.ANY)
    return pl.pallas_call(
        functools.partial(whiten_kernel, ncols, records),
        out_shape=jax.ShapeDtypeStruct((rows + TILE, width), jnp.bfloat16),
        in_specs=[pl.BlockSpec(memory_space=pltpu.SMEM), pl.BlockSpec(memory_space=pltpu.HBM)] + [anywhere] * 3,
        out_specs=pl.BlockSpec(memory_space=pltpu.VMEM),
        scratch_shapes=[
            pltpu.VMEM((rows, samples), jnp.bfloat16),
            pltpu.VMEM((1, taps), jnp.float32),
            pltpu.VMEM((1, bins), jnp.int32),
            pltpu.VMEM((1, slots), jnp.int32),
            pltpu.SemaphoreType.DMA((rows // CHUNK + 3,)),
        ],
        compiler_params=pltpu.CompilerParams(vmem_limit_bytes=SMALL),
        cost_estimate=pl.CostEstimate(
            flops=4 * rows * samples * width, bytes_accessed=2 * rows * samples, transcendentals=0
        ),
        name="whiten",
    )(
        reader_counts,
        raw_files.reshape(rows, samples),
        fir_taps.reshape(1, -1),
        band_bins.reshape(1, -1),
        file_channels.reshape(1, -1),
    )


def placing(packet, targets, records):
    rows = packet.shape[0] - TILE
    picks = []
    for group in range(rows // LANES):
        labels = packet[rows : rows + TILE, :].astype(jnp.float32)[group : group + 1]
        keys = labels * records + (iota((1, LANES), 1) % records).astype(jnp.float32)
        picks.append((targets == keys).astype(jnp.float32).astype(jnp.bfloat16))
    return jnp.concatenate(picks, axis=1)


def gather_rows(packets, targets, records):
    picks = jnp.concatenate([placing(p, targets, records) for p in packets], axis=1)
    data = jnp.concatenate([p[: p.shape[0] - TILE, :] for p in packets], axis=0)
    return dot(picks, data)


def own_kernel(records, *refs):
    packets, out = refs[:-1], refs[-1]
    count = out.shape[0]
    first = lax.axis_index("row") * count
    targets = (iota((count, 1), 0) + first).astype(jnp.float32)
    out[...] = gather_rows(packets, targets, records).astype(out.dtype)


def own_block(packets, records):
    vmem = pl.BlockSpec(memory_space=pltpu.VMEM)
    return pl.pallas_call(
        functools.partial(own_kernel, records),
        out_shape=jax.ShapeDtypeStruct((CH_DEV * records, packets[0].shape[1]), packets[0].dtype),
        in_specs=[vmem] * len(packets),
        out_specs=vmem,
        compiler_params=pltpu.CompilerParams(vmem_limit_bytes=SMALL),
        name="own",
    )(*packets)


def stack_piece(records, place, left, right_re, right_im, out, turned, tiles, sem):
    width = left.shape[1]
    half = width // 2
    count = right_re.shape[1]
    low = iota((1, width), 1) < half
    piece = left[...].astype(jnp.float32) * (1.0 / records)
    swapped = pltpu.roll(piece, half, 1)
    turned[0] = piece
    turned[1] = jnp.where(low, swapped, -swapped)

    @pl.loop(0, count // TILE)
    def _(j):
        rows = pl.ds(pl.multiple_of(j * TILE, TILE), TILE)
        res = [right_re[e, rows, :] for e in range(records)]
        ims = [right_im[e, rows, :] for e in range(records)]
        for k in range(CH_DEV):
            total = None
            for e in range(records):
                at = slice(k * records + e, k * records + e + 1)
                term = turned[0, at, :] * res[e] + turned[1, at, :] * ims[e]
                total = term if total is None else total + term
            tiles[k, rows, :] = total.astype(tiles.dtype)

    copy = pltpu.make_async_copy(tiles, out.at[pl.ds(place * CH_DEV, CH_DEV)], sem)
    copy.start()
    copy.wait()


def first_kernel(records, *refs):
    packets = refs[:-7]
    left, out, right_re, right_im, turned, tiles, sem = refs[-7:]
    width = left.shape[1]
    half = width // 2
    count = right_re.shape[1]
    low = iota((1, width), 1) < half
    for start in range(0, count, 64):
        block = min(64, count - start)
        row = iota((block * records, 1), 0)
        targets = ((row % block + start) * records + row // block).astype(jnp.float32)
        placed = gather_rows(packets, targets, records)
        swapped = pltpu.roll(placed, half, 1)
        res = jnp.where(low, placed, swapped)
        ims = jnp.where(low, swapped, placed)
        for record in range(records):
            right_re[record, start : start + block, :] = res[record * block : (record + 1) * block]
            right_im[record, start : start + block, :] = ims[record * block : (record + 1) * block]
    stack_piece(records, lax.axis_index("col"), left, right_re, right_im, out, turned, tiles, sem)


def next_kernel(records, shift, left, right_re, right_im, before, out, turned, tiles, sem):
    place = partner(lax.axis_index("col"), shift, before.shape[0] // CH_DEV, True)
    stack_piece(records, place, left, right_re, right_im, out, turned, tiles, sem)


def stacked(packets, lefts, records):
    nrows, ncols = len(packets), len(lefts)
    width = packets[0].shape[1]
    count = nrows * CH_DEV
    vmem = pl.BlockSpec(memory_space=pltpu.VMEM)
    anywhere = pl.BlockSpec(memory_space=pl.ANY)
    whole = jax.ShapeDtypeStruct((ncols * CH_DEV, count, width), jnp.bfloat16)
    right = jax.ShapeDtypeStruct((records, count, width), jnp.float32)
    scratch = [
        pltpu.VMEM((2, CH_DEV * records, width), jnp.float32),
        pltpu.VMEM((CH_DEV, count, width), jnp.bfloat16),
        pltpu.SemaphoreType.DMA,
    ]
    params = pltpu.CompilerParams(vmem_limit_bytes=SMALL)
    work = 4 * CH_DEV * count * width * records
    cost = pl.CostEstimate(flops=256 * work, bytes_accessed=whole.size * 2 // ncols, transcendentals=0)
    out, right_re, right_im = pl.pallas_call(
        functools.partial(first_kernel, records),
        out_shape=(whole, right, right),
        in_specs=[vmem] * (nrows + 1),
        out_specs=(anywhere, vmem, vmem),
        scratch_shapes=scratch,
        compiler_params=params,
        cost_estimate=cost,
        name="first",
    )(*packets, lefts[0][1])
    for shift, left in lefts[1:]:
        out = pl.pallas_call(
            functools.partial(next_kernel, records, shift),
            out_shape=whole,
            in_specs=[vmem] * 3 + [anywhere],
            out_specs=anywhere,
            scratch_shapes=scratch,
            input_output_aliases={3: 0},
            compiler_params=params,
            cost_estimate=cost,
            name="next",
        )(left, right_re, right_im, out)
    return out


def partner(index, shift, size, back=False):
    if size & (size - 1) == 0:
        return index ^ shift
    return (index + (size - shift if back else shift)) % size


def shifted(block, axis, order):
    size = lax.axis_size(axis)
    shifts = list(order) if len(order) == size - 1 else list(range(1, size))
    return [(0, block)] + [
        (s, lax.ppermute(block, axis, [(i, partner(i, s, size)) for i in range(size)])) for s in shifts
    ]


def on_device(raw_files, file_channels, reader_counts, fir_taps, band_bins):
    ncols = lax.axis_size("col")
    records = raw_files.shape[2]
    packet = whiten(raw_files, file_channels, reader_counts, fir_taps, band_bins, ncols)
    packets = [block for _, block in shifted(packet, "row", ROW_ORDER)]
    own = own_block(packets, records)
    lefts = shifted(own, "col", COL_ORDER)
    return stacked(packets, lefts, records)[:, None, :, :]


def solution(mesh):
    return jax.shard_map(
        on_device,
        mesh=mesh,
        in_specs=(
            P(("groups", "row"), "col", None, None),
            P(("groups", "row"), "col"),
            P(("groups", "row"), "col"),
            P(),
            P(),
        ),
        out_specs=P(("groups", "row"), "col", None, None),
        check_vma=False,
    )
```

time: 31.3 us -> 26.7 us (0.85)
  Pallas kernels: 12.9 us -> 8.59 us
  local copies, waits for them, and re-layouts: 1.23 us -> 3.83 us
  waiting for transfers between devices: 8.27 us -> 5.76 us
    pallas_call x2 -> x5, Pallas kernels: 11.3 us -> 8.42 us  [the longest x3 4.14 us: stacked(): pl.pallas_call(functools.partial(next_kernel, records, shift), out_shape=...]
    unnamed x12 -> x8, local copies, waits for them, and re-layouts: 1.23 us -> 3.83 us
    ppermute x6, waiting for transfers between devices: 8.27 us -> 5.76 us  [shifted(): lax.ppermute(block, axis, [(i, partner(i, s, size)) for i in range(size)])]
    pallas_call x1, Pallas kernels: 1.6 us -> 0.17 us  [own_block(): pl.pallas_call(functools.partial(own_kernel, records), out_shape=jax.Shap...]
  transfers between devices with their start and end apart: 6 -> 6, of which waited for: 6 -> 2; matrix products, arithmetic and copies ran while one was open for 0% -> 0% of each run, Pallas kernels for 0% -> 17%
where the time goes in v2:
time: 26.7 us; the launch traced here: 26.5 us
  Pallas kernels  8.59 us (32%)
  starting transfers between devices  7.63 us (29%)
  waiting for transfers between devices  5.76 us (22%)
  local copies, waits for them, and re-layouts  3.83 us (14%)
  between operations  0.74 us (3%)
    ppermute x6, starting transfers between devices, shifted(): lax.ppermute(block, axis, [(i, partner(i, s, size)) for i in range(size)])  7.63 us
    ppermute x6, waiting for transfers between devices, shifted(): lax.ppermute(block, axis, [(i, partner(i, s, size)) for i in range(size)])  5.76 us
    pallas_call x3, Pallas kernels, stacked(): pl.pallas_call(functools.partial(next_kernel, records, shift), out_shape=...  4.14 us
    unnamed x8, local copies, waits for them, and re-layouts  3.83 us
    pallas_call x1, Pallas kernels, whiten(): pl.pallas_call(functools.partial(whiten_kernel, ncols, records), out_shap...  2.61 us
    pallas_call x1, Pallas kernels, stacked(): pl.pallas_call(functools.partial(first_kernel, records), out_shape=(whole...  1.66 us
  transfers between devices with their start and end apart: 6, of which 2 were waited for; matrix products, arithmetic and copies ran while one was open for 0% of the time, Pallas kernels for 17%

profile of v2, /device:TPU:0, one launch (start us, length us, event | category | flops | bytes accessed | tf_op | source)
XLA Modules:
  0.0 26.5 jit_solution(11290645182862903820)
XLA Ops:
  0.7 0.0 copy-start
  0.7 1.9 %copy-done = bf16[16,1,8,12000]{3,2,1,0:T(8,128)(2,1)S(1)} copy-done((bf16[16,1,8,12000]{3,2,1,0:T(8,128)(2,1)S(1)}, bf16[16,1,8,12000]{3,2,1,0:T(8,128)(2,1)}, u32[]{:S(2)}) %copy-start) | copy-done | bytes 3072024
  2.5 0.0 copy-start.1
  2.5 0.7 %copy-done.1 = f32[32]{0:T(128)S(1)} copy-done((f32[32]{0:T(128)S(1)}, f32[32]{0:T(128)}, u32[]{:S(2)}) %copy-start.1) | copy-done | bytes 152
  3.2 0.0 copy-start.2
  3.2 0.7 %copy-done.2 = s32[64]{0:T(128)S(1)} copy-done((s32[64]{0:T(128)S(1)}, s32[64]{0:T(128)}, u32[]{:S(2)}) %copy-start.2) | copy-done | bytes 280
  3.8 0.0 copy-start.3
  3.8 0.7 %copy-done.3 = s32[16,1]{0,1:T(1,128)S(1)} copy-done((s32[16,1]{0,1:T(1,128)S(1)}, s32[16,1]{0,1:T(1,128)}, u32[]{:S(2)}) %copy-start.3) | copy-done | bytes 88
  4.5 2.6 %whiten.1.refs_0_ = bf16[144,128]{1,0:T(8,128)(2,1)S(1)} custom-call(s32[1,1]{1,0:T(1,128)S(6)} %copy.13.counts, bf16[128,12000]{1,0:T(8,128)(2,1)S(1)} %bitcast.7, f32[1,32]{1,0:T(1,128)S(1)} %bitcast.8, s32[1,64]{1,0:T(1,128)S(1)} %bitcast.9, s32[1,16]{1,0:T(1,128)S(1)} %bitcast.10), custom_call_target="tpu_custom_call" | custom-call | flops 786432000 | bytes 3072000 | tf_op jit(solution)/shard_map/whiten/pallas_call | solution.py:205
  7.1 3.1 %collective-permute-start = (bf16[144,128]{1,0:T(8,128)(2,1)S(1)}, bf16[144,128]{1,0:T(8,128)(2,1)S(1)}, u32[]{:S(2)}, u32[]{:S(2)}) collective-permute-start(bf16[144,128]{1,0:T(8,128)(2,1)S(1)} %whiten.1.refs_0_), channel_id=1, source_target_pairs={{0,4},{4,0},{8,12},{12,8},{1,5},{5,1},{9,13},{13,9},{2,6},{6,2},{1... | collective-permute-start | bytes 110600 | tf_op jit(solution)/shard_map/ppermute | solution.py:372
  10.2 2.6 %collective-permute-start.1 = (bf16[144,128]{1,0:T(8,128)(2,1)S(1)}, bf16[144,128]{1,0:T(8,128)(2,1)S(1)}, u32[]{:S(2)}, u32[]{:S(2)}) collective-permute-start(bf16[144,128]{1,0:T(8,128)(2,1)S(1)} %whiten.1.refs_0_), channel_id=1, source_target_pairs={{0,8},{4,12},{8,0},{12,4},{1,9},{5,13},{9,1},{13,5},{2,10},{6,14},... | collective-permute-start | bytes 110600 | tf_op jit(solution)/shard_map/ppermute | solution.py:372
  12.8 0.0 collective-permute-start.2
  12.8 0.0 collective-permute-done.refs_1_
  12.8 2.9 %collective-permute-done.1.refs_2_ = bf16[144,128]{1,0:T(8,128)(2,1)S(1)} collective-permute-done((bf16[144,128]{1,0:T(8,128)(2,1)S(1)}, bf16[144,128]{1,0:T(8,128)(2,1)S(1)}, u32[]{:S(2)}, u32[]{:S(2)}) %collective-permute-start.1) | collective-permute-done | bytes 36896 | tf_op jit(solution)/shard_map/ppermute | solution.py:372
  15.8 2.8 %collective-permute-done.2.refs_3_ = bf16[144,128]{1,0:T(8,128)(2,1)S(1)} collective-permute-done((bf16[144,128]{1,0:T(8,128)(2,1)S(1)}, bf16[144,128]{1,0:T(8,128)(2,1)S(1)}, u32[]{:S(2)}, u32[]{:S(2)}) %collective-permute-start.2) | collective-permute-done | bytes 36896 | tf_op jit(solution)/shard_map/ppermute | solution.py:372
  18.6 0.2 own.1.refs_4_
  18.8 0.1 collective-permute-start.5
  18.8 1.6 %collective-permute-start.4 = (bf16[128,128]{1,0:T(8,128)(2,1)S(1)}, bf16[128,128]{1,0:T(8,128)(2,1)S(1)}, u32[]{:S(2)}, u32[]{:S(2)}) collective-permute-start(bf16[128,128]{1,0:T(8,128)(2,1)S(1)} %own.1.refs_4_), channel_id=1, source_target_pairs={{0,2},{1,3},{2,0},{3,1},{4,6},{5,7},{6,4},{7,5},{8,10},{9,11},{10,... | collective-permute-start | bytes 98312 | tf_op jit(solution)/shard_map/ppermute | solution.py:372
  20.4 0.3 %collective-permute-start.3 = (bf16[128,128]{1,0:T(8,128)(2,1)S(1)}, bf16[128,128]{1,0:T(8,128)(2,1)S(1)}, u32[]{:S(2)}, u32[]{:S(2)}) collective-permute-start(bf16[128,128]{1,0:T(8,128)(2,1)S(1)} %own.1.refs_4_), channel_id=1, source_target_pairs={{0,3},{1,2},{2,1},{3,0},{4,7},{5,6},{6,5},{7,4},{8,11},{9,10},{10,... | collective-permute-start | bytes 98312 | tf_op jit(solution)/shard_map/ppermute | solution.py:372
  20.7 1.7 %first.1 = (bf16[64,64,128]{2,1,0:T(8,128)(2,1)}, f32[8,64,128]{2,1,0:T(8,128)S(1)}, f32[8,64,128]{2,1,0:T(8,128)S(1)}) custom-call(bf16[144,128]{1,0:T(8,128)(2,1)S(1)} %whiten.1.refs_0_, bf16[144,128]{1,0:T(8,128)(2,1)S(1)} %collective-permute-done.refs_1_, bf16[144,128]{1,0:T(8,128)(2,1)S(1)} %collective-permute-done.1.refs_2_, ...), custom_call_target="tpu_custom_call" | custom-call | flops 1073741824 | bytes 262144 | tf_op jit(solution)/shard_map/first/pallas_call | solution.py:337
  22.4 0.0 collective-permute-done.5.left
  22.4 1.4 %next.3.before = bf16[64,64,128]{2,1,0:T(8,128)(2,1)} custom-call(bf16[128,128]{1,0:T(8,128)(2,1)S(1)} %collective-permute-done.5.left, f32[8,64,128]{2,1,0:T(8,128)S(1)} %get-tuple-element.8.right_re, f32[8,64,128]{2,1,0:T(8,128)S(1)} %get-tuple-element.9.right_im, bf16[64,64,128]{2,1,0:T(8,128)(2,1)} %get-tuple-element.10.before), custom_call_target="tpu_custom_call", output_to_operand_aliasing={{}: (3, {})} | custom-call | flops 1073741824 | bytes 262144 | tf_op jit(solution)/shard_map/next/pallas_call | solution.py:348
  23.8 0.0 collective-permute-done.4.left
  23.8 1.4 %next.4.before = bf16[64,64,128]{2,1,0:T(8,128)(2,1)} custom-call(bf16[128,128]{1,0:T(8,128)(2,1)S(1)} %collective-permute-done.4.left, f32[8,64,128]{2,1,0:T(8,128)S(1)} %get-tuple-element.8.right_re, f32[8,64,128]{2,1,0:T(8,128)S(1)} %get-tuple-element.9.right_im, bf16[64,64,128]{2,1,0:T(8,128)(2,1)} %next.3.before), custom_call_target="tpu_custom_call", output_to_operand_aliasing={{}: (3, {})} | custom-call | flops 1073741824 | bytes 262144 | tf_op jit(solution)/shard_map/next/pallas_call | solution.py:348
  25.2 0.0 collective-permute-done.3.left
  25.2 1.4 %next.5 = bf16[64,64,128]{2,1,0:T(8,128)(2,1)} custom-call(bf16[128,128]{1,0:T(8,128)(2,1)S(1)} %collective-permute-done.3.left, f32[8,64,128]{2,1,0:T(8,128)S(1)} %get-tuple-element.8.right_re, f32[8,64,128]{2,1,0:T(8,128)S(1)} %get-tuple-element.9.right_im, bf16[64,64,128]{2,1,0:T(8,128)(2,1)} %next.4.before), custom_call_target="tpu_custom_call", output_to_operand_aliasing={{}: (3, {})} | custom-call | flops 1073741824 | bytes 262144 | tf_op jit(solution)/shard_map/next/pallas_call | solution.py:348
Async XLA Ops:
  0.7 1.9 %copy-start = (bf16[16,1,8,12000]{3,2,1,0:T(8,128)(2,1)S(1)}, bf16[16,1,8,12000]{3,2,1,0:T(8,128)(2,1)}, u32[]{:S(2)}) copy-start(bf16[16,1,8,12000]{3,2,1,0:T(8,128)(2,1)} %param.5) | copy-start | bytes 9216004
  2.5 0.7 %copy-start.1 = (f32[32]{0:T(128)S(1)}, f32[32]{0:T(128)}, u32[]{:S(2)}) copy-start(f32[32]{0:T(128)} %param.8) | copy-start | bytes 388
  3.2 0.7 %copy-start.2 = (s32[64]{0:T(128)S(1)}, s32[64]{0:T(128)}, u32[]{:S(2)}) copy-start(s32[64]{0:T(128)} %param.9) | copy-start | bytes 772
  3.8 0.7 %copy-start.3 = (s32[16,1]{0,1:T(1,128)S(1)}, s32[16,1]{0,1:T(1,128)}, u32[]{:S(2)}) copy-start(s32[16,1]{0,1:T(1,128)} %param.6) | copy-start | bytes 196
  7.1 5.7 %collective-permute-start = (bf16[144,128]{1,0:T(8,128)(2,1)S(1)}, bf16[144,128]{1,0:T(8,128)(2,1)S(1)}, u32[]{:S(2)}, u32[]{:S(2)}) collective-permute-start(bf16[144,128]{1,0:T(8,128)(2,1)S(1)} %whiten.1.refs_0_), channel_id=1, source_target_pairs={{0,4},{4,0},{8,12},{12,8},{1,5},{5,1},{9,13},{13,9},{2,6},{6,2},{1... | collective-permute-start | bytes 110600 | tf_op jit(solution)/shard_map/ppermute | solution.py:372
  10.2 5.5 %collective-permute-start.1 = (bf16[144,128]{1,0:T(8,128)(2,1)S(1)}, bf16[144,128]{1,0:T(8,128)(2,1)S(1)}, u32[]{:S(2)}, u32[]{:S(2)}) collective-permute-start(bf16[144,128]{1,0:T(8,128)(2,1)S(1)} %whiten.1.refs_0_), channel_id=1, source_target_pairs={{0,8},{4,12},{8,0},{12,4},{1,9},{5,13},{9,1},{13,5},{2,10},{6,14},... | collective-permute-start | bytes 110600 | tf_op jit(solution)/shard_map/ppermute | solution.py:372
  12.8 5.8 %collective-permute-start.2 = (bf16[144,128]{1,0:T(8,128)(2,1)S(1)}, bf16[144,128]{1,0:T(8,128)(2,1)S(1)}, u32[]{:S(2)}, u32[]{:S(2)}) collective-permute-start(bf16[144,128]{1,0:T(8,128)(2,1)S(1)} %whiten.1.refs_0_), channel_id=1, source_target_pairs={{0,12},{4,8},{8,4},{12,0},{1,13},{5,9},{9,5},{13,1},{2,14},{6,10},... | collective-permute-start | bytes 110600 | tf_op jit(solution)/shard_map/ppermute | solution.py:372
  18.8 3.6 %collective-permute-start.5 = (bf16[128,128]{1,0:T(8,128)(2,1)S(1)}, bf16[128,128]{1,0:T(8,128)(2,1)S(1)}, u32[]{:S(2)}, u32[]{:S(2)}) collective-permute-start(bf16[128,128]{1,0:T(8,128)(2,1)S(1)} %own.1.refs_4_), channel_id=1, source_target_pairs={{0,1},{1,0},{2,3},{3,2},{4,5},{5,4},{6,7},{7,6},{8,9},{9,8},{10,11... | collective-permute-start | bytes 98312 | tf_op jit(solution)/shard_map/ppermute | solution.py:372
  18.8 4.9 %collective-permute-start.4 = (bf16[128,128]{1,0:T(8,128)(2,1)S(1)}, bf16[128,128]{1,0:T(8,128)(2,1)S(1)}, u32[]{:S(2)}, u32[]{:S(2)}) collective-permute-start(bf16[128,128]{1,0:T(8,128)(2,1)S(1)} %own.1.refs_4_), channel_id=1, source_target_pairs={{0,2},{1,3},{2,0},{3,1},{4,6},{5,7},{6,4},{7,5},{8,10},{9,11},{10,... | collective-permute-start | bytes 98312 | tf_op jit(solution)/shard_map/ppermute | solution.py:372
  20.4 4.8 %collective-permute-start.3 = (bf16[128,128]{1,0:T(8,128)(2,1)S(1)}, bf16[128,128]{1,0:T(8,128)(2,1)S(1)}, u32[]{:S(2)}, u32[]{:S(2)}) collective-permute-start(bf16[128,128]{1,0:T(8,128)(2,1)S(1)} %own.1.refs_4_), channel_id=1, source_target_pairs={{0,3},{1,2},{2,1},{3,0},{4,7},{5,6},{6,5},{7,4},{8,11},{9,10},{10,... | collective-permute-start | bytes 98312 | tf_op jit(solution)/shard_map/ppermute | solution.py:372

commit v3 on v2

--- a/solution.py
+++ b/solution.py
@@ -49,7 +49,9 @@
     return lax.broadcasted_iota(jnp.int32, shape, axis)
 
 
-def whiten_kernel(ncols, records, counts, raw, taps_in, bins_in, channels_in, out, held, taps, bins, channels, sems):
+def whiten_kernel(ncols, records, *refs):
+    (raw, taps_in, bins_in, channels_in), counts, refs = refs[:4], refs[4:-6], refs[-6:]
+    out, held, taps, bins, channels, sems = refs
     rows, samples = raw.shape
     taps_count = taps.shape[1]
     length = samples // DEC
@@ -142,8 +144,10 @@
         spectra = along * sign - pltpu.roll(across, half, 1)
         power = jnp.mean(spectra * spectra, axis=1, keepdims=True)
         white = spectra / jnp.sqrt(power + 1e-06)
-        slot = (iota((CHUNK, 1), 0) + index * CHUNK) // records
-        out[index * CHUNK : (index + 1) * CHUNK, :] = jnp.where(slot < counts[0, 0], white, 0.0).astype(out.dtype)
+        if counts:
+            slot = (iota((CHUNK, 1), 0) + index * CHUNK) // records
+            white = jnp.where(slot < counts[0][0, 0], white, 0.0)
+        out[index * CHUNK : (index + 1) * CHUNK, :] = white.astype(out.dtype)
 
     def every_chunk(*accs):
         along = across = None
@@ -186,7 +190,9 @@
     pl.run_scoped(every_chunk, *accs)
     owner = channels[...] // (CH_DEV * ncols)
     local = owner * CH_DEV + channels[...] % CH_DEV
-    local = jnp.where(iota((1, slots), 1) < counts[0, 0], local, -1).astype(jnp.float32)
+    if counts:
+        local = jnp.where(iota((1, slots), 1) < counts[0][0, 0], local, -1)
+    local = local.astype(jnp.float32)
     local = jnp.broadcast_to(
         jnp.concatenate([local, jnp.zeros((1, LANES - slots), jnp.float32)], axis=1), (TILE, LANES)
     )
@@ -201,11 +207,12 @@
     bins = band_bins.shape[0]
     taps = fir_taps.shape[0]
     width = 2 * bins
+    counts = [] if slots == CH_DEV else [reader_counts]
     anywhere = pl.BlockSpec(memory_space=pl.ANY)
     return pl.pallas_call(
         functools.partial(whiten_kernel, ncols, records),
         out_shape=jax.ShapeDtypeStruct((rows + TILE, width), jnp.bfloat16),
-        in_specs=[pl.BlockSpec(memory_space=pltpu.SMEM), pl.BlockSpec(memory_space=pltpu.HBM)] + [anywhere] * 3,
+        in_specs=[anywhere] * 4 + [pl.BlockSpec(memory_space=pltpu.SMEM)] * len(counts),
         out_specs=pl.BlockSpec(memory_space=pltpu.VMEM),
         scratch_shapes=[
             pltpu.VMEM((rows, samples), jnp.bfloat16),
@@ -220,11 +227,16 @@
         ),
         name="whiten",
     )(
-        reader_counts,
-        raw_files.reshape(rows, samples),
-        fir_taps.reshape(1, -1),
-        band_bins.reshape(1, -1),
-        file_channels.reshape(1, -1),
+        *(
+            pltpu.with_memory_space_constraint(x, pltpu.HBM)
+            for x in (
+                raw_files.reshape(rows, samples),
+                fir_taps.reshape(1, -1),
+                band_bins.reshape(1, -1),
+                file_channels.reshape(1, -1),
+            )
+        ),
+        *counts,
     )
 
 
@@ -264,37 +276,41 @@
     )(*packets)
 
 
-def stack_piece(records, place, left, right_re, right_im, out, turned, tiles, sem):
-    width = left.shape[1]
+def stack_pieces(records, places, lefts, right_re, right_im, out, turned, tiles, sems):
+    width = lefts[0].shape[1]
     half = width // 2
     count = right_re.shape[1]
     low = iota((1, width), 1) < half
-    piece = left[...].astype(jnp.float32) * (1.0 / records)
-    swapped = pltpu.roll(piece, half, 1)
-    turned[0] = piece
-    turned[1] = jnp.where(low, swapped, -swapped)
-
-    @pl.loop(0, count // TILE)
-    def _(j):
-        rows = pl.ds(pl.multiple_of(j * TILE, TILE), TILE)
-        res = [right_re[e, rows, :] for e in range(records)]
-        ims = [right_im[e, rows, :] for e in range(records)]
-        for k in range(CH_DEV):
-            total = None
-            for e in range(records):
-                at = slice(k * records + e, k * records + e + 1)
-                term = turned[0, at, :] * res[e] + turned[1, at, :] * ims[e]
-                total = term if total is None else total + term
-            tiles[k, rows, :] = total.astype(tiles.dtype)
-
-    copy = pltpu.make_async_copy(tiles, out.at[pl.ds(place * CH_DEV, CH_DEV)], sem)
-    copy.start()
-    copy.wait()
+    copies = []
+    for index, (place, left) in enumerate(zip(places, lefts)):
+        piece = left[...].astype(jnp.float32) * (1.0 / records)
+        swapped = pltpu.roll(piece, half, 1)
+        turned[index, 0] = piece
+        turned[index, 1] = jnp.where(low, swapped, -swapped)
+
+        @pl.loop(0, count // TILE)
+        def _(j):
+            rows = pl.ds(pl.multiple_of(j * TILE, TILE), TILE)
+            res = [right_re[e, rows, :] for e in range(records)]
+            ims = [right_im[e, rows, :] for e in range(records)]
+            for k in range(CH_DEV):
+                total = None
+                for e in range(records):
+                    at = slice(k * records + e, k * records + e + 1)
+                    term = turned[index, 0, at, :] * res[e] + turned[index, 1, at, :] * ims[e]
+                    total = term if total is None else total + term
+                tiles[index, k, rows, :] = total.astype(tiles.dtype)
+
+        target = out.at[pl.ds(place * CH_DEV, CH_DEV)]
+        copies.append(pltpu.make_async_copy(tiles.at[index], target, sems.at[index]))
+        copies[-1].start()
+    for copy in copies:
+        copy.wait()
 
 
 def first_kernel(records, *refs):
     packets = refs[:-7]
-    left, out, right_re, right_im, turned, tiles, sem = refs[-7:]
+    left, out, right_re, right_im, turned, tiles, sems = refs[-7:]
     width = left.shape[1]
     half = width // 2
     count = right_re.shape[1]
@@ -310,12 +326,15 @@
         for record in range(records):
             right_re[record, start : start + block, :] = res[record * block : (record + 1) * block]
             right_im[record, start : start + block, :] = ims[record * block : (record + 1) * block]
-    stack_piece(records, lax.axis_index("col"), left, right_re, right_im, out, turned, tiles, sem)
-
-
-def next_kernel(records, shift, left, right_re, right_im, before, out, turned, tiles, sem):
-    place = partner(lax.axis_index("col"), shift, before.shape[0] // CH_DEV, True)
-    stack_piece(records, place, left, right_re, right_im, out, turned, tiles, sem)
+    stack_pieces(records, [lax.axis_index("col")], [left], right_re, right_im, out, turned, tiles, sems)
+
+
+def rest_kernel(records, shifts, *refs):
+    lefts = refs[: len(shifts)]
+    right_re, right_im, before, out, turned, tiles, sems = refs[len(shifts) :]
+    mine = lax.axis_index("col")
+    places = [partner(mine, shift, before.shape[0] // CH_DEV, True) for shift in shifts]
+    stack_pieces(records, places, lefts, right_re, right_im, out, turned, tiles, sems)
 
 
 def stacked(packets, lefts, records):
@@ -326,37 +345,43 @@
     anywhere = pl.BlockSpec(memory_space=pl.ANY)
     whole = jax.ShapeDtypeStruct((ncols * CH_DEV, count, width), jnp.bfloat16)
     right = jax.ShapeDtypeStruct((records, count, width), jnp.float32)
-    scratch = [
-        pltpu.VMEM((2, CH_DEV * records, width), jnp.float32),
-        pltpu.VMEM((CH_DEV, count, width), jnp.bfloat16),
-        pltpu.SemaphoreType.DMA,
-    ]
     params = pltpu.CompilerParams(vmem_limit_bytes=SMALL)
-    work = 4 * CH_DEV * count * width * records
-    cost = pl.CostEstimate(flops=256 * work, bytes_accessed=whole.size * 2 // ncols, transcendentals=0)
+
+    def scratch(pieces):
+        return [
+            pltpu.VMEM((pieces, 2, CH_DEV * records, width), jnp.float32),
+            pltpu.VMEM((pieces, CH_DEV, count, width), jnp.bfloat16),
+            pltpu.SemaphoreType.DMA((pieces,)),
+        ]
+
+    def cost(pieces):
+        work = 4 * CH_DEV * count * width * records * pieces
+        return pl.CostEstimate(
+            flops=256 * work, bytes_accessed=whole.size * 2 * pieces // ncols, transcendentals=0
+        )
+
     out, right_re, right_im = pl.pallas_call(
         functools.partial(first_kernel, records),
         out_shape=(whole, right, right),
         in_specs=[vmem] * (nrows + 1),
         out_specs=(anywhere, vmem, vmem),
-        scratch_shapes=scratch,
+        scratch_shapes=scratch(1),
         compiler_params=params,
-        cost_estimate=cost,
+        cost_estimate=cost(1),
         name="first",
     )(*packets, lefts[0][1])
-    for shift, left in lefts[1:]:
-        out = pl.pallas_call(
-            functools.partial(next_kernel, records, shift),
-            out_shape=whole,
-            in_specs=[vmem] * 3 + [anywhere],
-            out_specs=anywhere,
-            scratch_shapes=scratch,
-            input_output_aliases={3: 0},
-            compiler_params=params,
-            cost_estimate=cost,
-            name="next",
-        )(left, right_re, right_im, out)
-    return out
+    others = lefts[1:]
+    return pl.pallas_call(
+        functools.partial(rest_kernel, records, [shift for shift, _ in others]),
+        out_shape=whole,
+        in_specs=[vmem] * (len(others) + 2) + [anywhere],
+        out_specs=anywhere,
+        scratch_shapes=scratch(len(others)),
+        input_output_aliases={len(others) + 2: 0},
+        compiler_params=params,
+        cost_estimate=cost(len(others)),
+        name="rest",
+    )(*[left for _, left in others], right_re, right_im, out)
 
 
 def partner(index, shift, size, back=False):

time: 26.7 us -> 20.2 us (0.76)
  local copies, waits for them, and re-layouts: 3.83 us -> 0 us
  waiting for transfers between devices: 5.76 us -> 4.71 us
  Pallas kernels: 8.59 us -> 7.56 us
  between operations: 0.74 us -> 0.04 us
    unnamed x8 -> x0, local copies, waits for them, and re-layouts: 3.83 us -> none
    pallas_call x3 -> x1, Pallas kernels: 4.14 us -> 2.8 us  [stacked(): pl.pallas_call(functools.partial(rest_kernel, records, [shift for shift,...]
    ppermute x6, waiting for transfers between devices: 5.76 us -> 4.71 us  [shifted(): lax.ppermute(block, axis, [(i, partner(i, s, size)) for i in range(size)])]
    pallas_call x1, Pallas kernels: 2.61 us -> 2.9 us  [whiten(): pl.pallas_call(functools.partial(whiten_kernel, ncols, records), out_shap...]
  transfers between devices with their start and end apart: 6 -> 6, of which waited for: 2 -> 4; matrix products, arithmetic and copies ran while one was open for 0% -> 0% of each run, Pallas kernels for 17% -> 8%
where the time goes in v3:
time: 20.2 us; the launch traced here: 20 us
  starting transfers between devices  7.7 us (38%)
  Pallas kernels  7.56 us (37%)
  waiting for transfers between devices  4.71 us (23%)
    ppermute x6, starting transfers between devices, shifted(): lax.ppermute(block, axis, [(i, partner(i, s, size)) for i in range(size)])  7.7 us
    ppermute x6, waiting for transfers between devices, shifted(): lax.ppermute(block, axis, [(i, partner(i, s, size)) for i in range(size)])  4.71 us
    pallas_call x1, Pallas kernels, whiten(): pl.pallas_call(functools.partial(whiten_kernel, ncols, records), out_shap...  2.9 us
    pallas_call x1, Pallas kernels, stacked(): pl.pallas_call(functools.partial(rest_kernel, records, [shift for shift,...  2.8 us
    pallas_call x1, Pallas kernels, stacked(): pl.pallas_call(functools.partial(first_kernel, records), out_shape=(whole...  1.68 us
  transfers between devices with their start and end apart: 6, of which 4 were waited for; matrix products, arithmetic and copies ran while one was open for 0% of the time, Pallas kernels for 8%

profile of v3, /device:TPU:0, one launch (start us, length us, event | category | flops | bytes accessed | tf_op | source)
XLA Modules:
  0.0 20.0 jit_solution(10332657492263405616)
XLA Ops:
  0.0 2.9 %whiten.1.refs_0_ = bf16[144,128]{1,0:T(8,128)(2,1)S(1)} custom-call(bf16[128,12000]{1,0:T(8,128)(2,1)} %bitcast.7, f32[1,32]{1,0:T(1,128)} %bitcast.8, s32[1,64]{1,0:T(1,128)} %bitcast.9, s32[1,16]{1,0:T(1,128)} %bitcast.10), custom_call_target="tpu_custom_call" | custom-call | flops 786432000 | bytes 3072000 | tf_op jit(solution)/shard_map/whiten/pallas_call | solution.py:212
  2.9 5.1 %collective-permute-start.2 = (bf16[144,128]{1,0:T(8,128)(2,1)S(1)}, bf16[144,128]{1,0:T(8,128)(2,1)S(1)}, u32[]{:S(2)}, u32[]{:S(2)}) collective-permute-start(bf16[144,128]{1,0:T(8,128)(2,1)S(1)} %whiten.1.refs_0_), channel_id=1, source_target_pairs={{0,12},{4,8},{8,4},{12,0},{1,13},{5,9},{9,5},{13,1},{2,14},{6,10},... | collective-permute-start | bytes 110600 | tf_op jit(solution)/shard_map/ppermute | solution.py:397
  8.0 0.0 collective-permute-start.1
  8.1 0.6 %collective-permute-start = (bf16[144,128]{1,0:T(8,128)(2,1)S(1)}, bf16[144,128]{1,0:T(8,128)(2,1)S(1)}, u32[]{:S(2)}, u32[]{:S(2)}) collective-permute-start(bf16[144,128]{1,0:T(8,128)(2,1)S(1)} %whiten.1.refs_0_), channel_id=1, source_target_pairs={{0,4},{4,0},{8,12},{12,8},{1,5},{5,1},{9,13},{13,9},{2,6},{6,2},{1... | collective-permute-start | bytes 110600 | tf_op jit(solution)/shard_map/ppermute | solution.py:397
  8.7 1.3 %collective-permute-done.2.refs_3_ = bf16[144,128]{1,0:T(8,128)(2,1)S(1)} collective-permute-done((bf16[144,128]{1,0:T(8,128)(2,1)S(1)}, bf16[144,128]{1,0:T(8,128)(2,1)S(1)}, u32[]{:S(2)}, u32[]{:S(2)}) %collective-permute-start.2) | collective-permute-done | bytes 36896 | tf_op jit(solution)/shard_map/ppermute | solution.py:397
  10.0 2.9 %collective-permute-done.1.refs_2_ = bf16[144,128]{1,0:T(8,128)(2,1)S(1)} collective-permute-done((bf16[144,128]{1,0:T(8,128)(2,1)S(1)}, bf16[144,128]{1,0:T(8,128)(2,1)S(1)}, u32[]{:S(2)}, u32[]{:S(2)}) %collective-permute-start.1) | collective-permute-done | bytes 36896 | tf_op jit(solution)/shard_map/ppermute | solution.py:397
  12.9 0.0 collective-permute-done.refs_1_
  12.9 0.2 own.1.refs_4_
  13.1 0.1 collective-permute-start.5
  13.2 1.6 %collective-permute-start.4 = (bf16[128,128]{1,0:T(8,128)(2,1)S(1)}, bf16[128,128]{1,0:T(8,128)(2,1)S(1)}, u32[]{:S(2)}, u32[]{:S(2)}) collective-permute-start(bf16[128,128]{1,0:T(8,128)(2,1)S(1)} %own.1.refs_4_), channel_id=1, source_target_pairs={{0,2},{1,3},{2,0},{3,1},{4,6},{5,7},{6,4},{7,5},{8,10},{9,11},{10,... | collective-permute-start | bytes 98312 | tf_op jit(solution)/shard_map/ppermute | solution.py:397
  14.7 0.3 %collective-permute-start.3 = (bf16[128,128]{1,0:T(8,128)(2,1)S(1)}, bf16[128,128]{1,0:T(8,128)(2,1)S(1)}, u32[]{:S(2)}, u32[]{:S(2)}) collective-permute-start(bf16[128,128]{1,0:T(8,128)(2,1)S(1)} %own.1.refs_4_), channel_id=1, source_target_pairs={{0,1},{1,0},{2,3},{3,2},{4,5},{5,4},{6,7},{7,6},{8,9},{9,8},{10,11... | collective-permute-start | bytes 98312 | tf_op jit(solution)/shard_map/ppermute | solution.py:397
  15.0 1.7 %first.1 = (bf16[64,64,128]{2,1,0:T(8,128)(2,1)}, f32[8,64,128]{2,1,0:T(8,128)S(1)}, f32[8,64,128]{2,1,0:T(8,128)S(1)}) custom-call(bf16[144,128]{1,0:T(8,128)(2,1)S(1)} %whiten.1.refs_0_, bf16[144,128]{1,0:T(8,128)(2,1)S(1)} %collective-permute-done.refs_1_, bf16[144,128]{1,0:T(8,128)(2,1)S(1)} %collective-permute-done.1.refs_2_, ...), custom_call_target="tpu_custom_call" | custom-call | flops 1073741824 | bytes 262144 | tf_op jit(solution)/shard_map/first/pallas_call | solution.py:363
  16.7 0.1 collective-permute-done.5.refs_2_
  16.8 0.4 %collective-permute-done.4.refs_1_ = bf16[128,128]{1,0:T(8,128)(2,1)S(1)} collective-permute-done((bf16[128,128]{1,0:T(8,128)(2,1)S(1)}, bf16[128,128]{1,0:T(8,128)(2,1)S(1)}, u32[]{:S(2)}, u32[]{:S(2)}) %collective-permute-start.4) | collective-permute-done | bytes 32800 | tf_op jit(solution)/shard_map/ppermute | solution.py:397
  17.2 0.0 collective-permute-done.3.refs_0_
  17.2 2.8 %rest.1 = bf16[64,64,128]{2,1,0:T(8,128)(2,1)} custom-call(bf16[128,128]{1,0:T(8,128)(2,1)S(1)} %collective-permute-done.3.refs_0_, bf16[128,128]{1,0:T(8,128)(2,1)S(1)} %collective-permute-done.4.refs_1_, bf16[128,128]{1,0:T(8,128)(2,1)S(1)} %collective-permute-done.5.refs_2_, ...), custom_call_target="tpu_custom_call", output_to_operand_aliasing={{}: (5, {})} | custom-call | flops 3221225472 | bytes 786432 | tf_op jit(solution)/shard_map/rest/pallas_call | solution.py:374
Async XLA Ops:
  2.9 7.1 %collective-permute-start.2 = (bf16[144,128]{1,0:T(8,128)(2,1)S(1)}, bf16[144,128]{1,0:T(8,128)(2,1)S(1)}, u32[]{:S(2)}, u32[]{:S(2)}) collective-permute-start(bf16[144,128]{1,0:T(8,128)(2,1)S(1)} %whiten.1.refs_0_), channel_id=1, source_target_pairs={{0,12},{4,8},{8,4},{12,0},{1,13},{5,9},{9,5},{13,1},{2,14},{6,10},... | collective-permute-start | bytes 110600 | tf_op jit(solution)/shard_map/ppermute | solution.py:397
  8.0 4.9 %collective-permute-start.1 = (bf16[144,128]{1,0:T(8,128)(2,1)S(1)}, bf16[144,128]{1,0:T(8,128)(2,1)S(1)}, u32[]{:S(2)}, u32[]{:S(2)}) collective-permute-start(bf16[144,128]{1,0:T(8,128)(2,1)S(1)} %whiten.1.refs_0_), channel_id=1, source_target_pairs={{0,8},{4,12},{8,0},{12,4},{1,9},{5,13},{9,1},{13,5},{2,10},{6,14},... | collective-permute-start | bytes 110600 | tf_op jit(solution)/shard_map/ppermute | solution.py:397
  8.1 4.9 %collective-permute-start = (bf16[144,128]{1,0:T(8,128)(2,1)S(1)}, bf16[144,128]{1,0:T(8,128)(2,1)S(1)}, u32[]{:S(2)}, u32[]{:S(2)}) collective-permute-start(bf16[144,128]{1,0:T(8,128)(2,1)S(1)} %whiten.1.refs_0_), channel_id=1, source_target_pairs={{0,4},{4,0},{8,12},{12,8},{1,5},{5,1},{9,13},{13,9},{2,6},{6,2},{1... | collective-permute-start | bytes 110600 | tf_op jit(solution)/shard_map/ppermute | solution.py:397
  13.1 3.7 %collective-permute-start.5 = (bf16[128,128]{1,0:T(8,128)(2,1)S(1)}, bf16[128,128]{1,0:T(8,128)(2,1)S(1)}, u32[]{:S(2)}, u32[]{:S(2)}) collective-permute-start(bf16[128,128]{1,0:T(8,128)(2,1)S(1)} %own.1.refs_4_), channel_id=1, source_target_pairs={{0,3},{1,2},{2,1},{3,0},{4,7},{5,6},{6,5},{7,4},{8,11},{9,10},{10,... | collective-permute-start | bytes 98312 | tf_op jit(solution)/shard_map/ppermute | solution.py:397
  13.2 4.0 %collective-permute-start.4 = (bf16[128,128]{1,0:T(8,128)(2,1)S(1)}, bf16[128,128]{1,0:T(8,128)(2,1)S(1)}, u32[]{:S(2)}, u32[]{:S(2)}) collective-permute-start(bf16[128,128]{1,0:T(8,128)(2,1)S(1)} %own.1.refs_4_), channel_id=1, source_target_pairs={{0,2},{1,3},{2,0},{3,1},{4,6},{5,7},{6,4},{7,5},{8,10},{9,11},{10,... | collective-permute-start | bytes 98312 | tf_op jit(solution)/shard_map/ppermute | solution.py:397
  14.7 2.5 %collective-permute-start.3 = (bf16[128,128]{1,0:T(8,128)(2,1)S(1)}, bf16[128,128]{1,0:T(8,128)(2,1)S(1)}, u32[]{:S(2)}, u32[]{:S(2)}) collective-permute-start(bf16[128,128]{1,0:T(8,128)(2,1)S(1)} %own.1.refs_4_), channel_id=1, source_target_pairs={{0,1},{1,0},{2,3},{3,2},{4,5},{5,4},{6,7},{7,6},{8,9},{9,8},{10,11... | collective-permute-start | bytes 98312 | tf_op jit(solution)/shard_map/ppermute | solution.py:397

commit v4 on v3

v4 whole, which is shorter than its diff:
```python
import functools
import math

import jax
import jax.numpy as jnp
from jax import lax
from jax.experimental import pallas as pl
from jax.experimental.pallas import tpu as pltpu
from jax.sharding import PartitionSpec as P

CH_DEV = 16
DEC = 4
SPAN = 1024
LANES = 128
TILE = 16
BLOCK = 64
EARLY = 1
CHAINS = 2
GROUP = 128
HALF = 64
CUTS = (4, 8)
MXU = 256
SMALL = 16 << 20
ROW_ORDER = (1, 2, 3)
COL_ORDER = (1, 2, 3)
USE_ORDER = (1, 2, 3)
SIN = (6.283185307, -41.341702147, 81.60523051, -76.704495669, 42.014104466, -14.423992009)


def split(x):
    high = x.astype(jnp.bfloat16)
    return high, (x - high.astype(jnp.float32)).astype(jnp.bfloat16)


def turn_cos(steps, length):
    steps = steps - jnp.round(steps * (1.0 / length)) * length
    gap = 0.25 - jnp.abs(steps * (1.0 / length))
    square = gap * gap
    value = jnp.full_like(gap, SIN[-1])
    for term in SIN[-2::-1]:
        value = value * square + term
    return value * gap


def dot(a, b):
    return jnp.dot(a, b, preferred_element_type=jnp.float32)


def dot_t(a, b):
    return lax.dot_general(a, b, (((1,), (1,)), ((), ())), preferred_element_type=jnp.float32)


def iota(shape, axis):
    return lax.broadcasted_iota(jnp.int32, shape, axis)


def whiten_kernel(ncols, records, *refs):
    (raw, taps_in, bins_in, channels_in), counts, refs = refs[:4], refs[4:-8], refs[-8:]
    out, held, taps, bins, channels, waves, ordered, sems = refs
    rows, samples = raw.shape
    taps_count = taps.shape[1]
    length = samples // DEC
    blocks = (samples + SPAN - 1) // SPAN
    sets = [range(a, min(b, blocks)) for a, b in zip((0,) + CUTS, CUTS + (blocks,)) if a < blocks]
    small = []
    for index, (source, target) in enumerate(((taps_in, taps), (bins_in, bins), (channels_in, channels))):
        small.append(pltpu.make_async_copy(source, target, sems.at[index]))
        small[-1].start()
    copies = []
    for index, group in enumerate(sets):
        start = group[0] * SPAN
        part = pl.ds(start, min(len(group) * SPAN, samples - start))
        copies.append(pltpu.make_async_copy(raw.at[:, part], held.at[:, part], sems.at[3 + index]))
        copies[-1].start()
    for copy in small:
        copy.wait()
    width = out.shape[1]
    half = width // 2
    before = taps_count // DEC - 1
    tiles = SPAN // LANES
    depth = (LANES // DEC + before + TILE - 1) // TILE * TILE
    quarter = 0.25 * length
    base = bins[...].astype(jnp.float32)
    band = jnp.concatenate([base, base], axis=1)
    turn_at, back_at = depth, depth + tiles
    cos_at = depth + 2 * tiles
    sin_at = cos_at + TILE
    lower = iota((sin_at + TILE, width), 1) // half
    row = iota((sin_at + TILE, width), 0)
    steps = jnp.where(row < turn_at, row - before, (row - turn_at) % tiles * (LANES // DEC))
    steps = jnp.where(row < cos_at, steps, (row - cos_at) % TILE * (SPAN // DEC))
    shift = jnp.where(row < turn_at, lower, 0)
    shift = jnp.where((row >= back_at) & (row < cos_at), 1, shift)
    shift = jnp.where(row >= sin_at, 1, shift)
    values = turn_cos(steps.astype(jnp.float32) * band - shift.astype(jnp.float32) * quarter, length)
    flip = (row >= back_at) & (row < cos_at) & (lower == 0)
    waves[...] = jnp.where(flip, -values, values)
    gap = iota((LANES, LANES), 0) - DEC * (iota((LANES, LANES), 1) - before)
    lane_taps = jnp.concatenate([taps[...], jnp.zeros((1, LANES - taps_count), jnp.float32)], axis=1)
    lane_taps = jnp.broadcast_to(lane_taps, (LANES, LANES))
    banded = jnp.take_along_axis(lane_taps, jnp.clip(gap, 0, taps_count - 1), axis=1)
    banded = jnp.where((gap >= 0) & (gap < taps_count), banded, 0.0)
    edge_rows = (DEC * before + TILE - 1) // TILE * TILE
    early = jnp.where(iota((edge_rows, LANES), 1) < before, -banded[:edge_rows], 0.0)
    filters = jnp.concatenate(split(jnp.concatenate([banded, early], axis=0)), axis=1)
    wave_high, wave_low = split(waves[:depth, :])
    space = jnp.zeros((LANES - depth, 2 * width), jnp.bfloat16)
    rhs = jnp.concatenate(
        [
            jnp.concatenate([wave_high, wave_low], axis=1),
            space,
            jnp.concatenate([wave_high, jnp.zeros_like(wave_low)], axis=1),
            space,
        ],
        axis=0,
    )

    def product(acc):
        pltpu.matmul_push_rhs(rhs, 0, 0)
        pltpu.matmul_acc_lhs(acc, filters, load_staged_rhs=0)
        both = pltpu.matmul_pop(acc)
        return both[:, :width] + both[:, width:]

    filtered = pl.run_scoped(product, pltpu.ACC(0)((LANES + edge_rows, MXU), jnp.float32))
    first, edge = filtered[:LANES], filtered[LANES:]
    swapped = pltpu.roll(first, half, 1)
    half_tables = []
    for index in range(0, tiles, MXU // LANES):
        pieces = []
        for tile in range(index, index + MXU // LANES):
            turned = first * waves[turn_at + tile : turn_at + tile + 1, :]
            turned = turned + swapped * waves[back_at + tile : back_at + tile + 1, :]
            pieces.append(turned if tile else first)
        half_tables.append(jnp.concatenate(split(jnp.concatenate(pieces, axis=0)), axis=1))
    edge = jnp.concatenate(split(edge), axis=1)
    edge = jnp.concatenate([edge, jnp.zeros((MXU - edge_rows, 2 * width), jnp.bfloat16)], axis=0)
    sign = jnp.where(iota((1, width), 1) < half, 1.0, -1.0)
    slots = rows // records

    def piece(part, start):
        size = min(MXU, samples - start)
        block = held[part, start : start + size]
        if size < MXU:
            block = jnp.concatenate([block, jnp.zeros((HALF, MXU - size), block.dtype)], axis=1)
        return block

    accs = [
        pltpu.ACC(block % 2)((HALF, 2 * width), jnp.float32) for block in range(blocks) for _ in range(GROUP // HALF)
    ]

    def finish(top, along, across):
        spectra = along * sign - pltpu.roll(across, half, 1)
        power = jnp.mean(spectra * spectra, axis=1, keepdims=True)
        white = spectra / jnp.sqrt(power + 1e-06)
        if counts:
            slot = (iota((HALF, 1), 0) + top) // records
            white = jnp.where(slot < counts[0][0, 0], white, 0.0)
        for index in range(HALF // records):
            turned = pl.ds(top // records + index, records, stride=slots)
            ordered[turned, :] = white[index * records : (index + 1) * records]

    steps_count = SPAN // MXU

    def used(members, step, unit):
        return [b for b in members if b % 2 == unit and b * SPAN + step * MXU < samples]

    orders = [[step for members in sets for step in range(steps_count) if used(members, step, unit)] for unit in range(2)]

    def push_next(unit, pushed):
        if pushed[unit] < len(orders[unit]):
            pltpu.matmul_push_rhs(half_tables[orders[unit][pushed[unit]]], pushed[unit] % 2, unit)
        pushed[unit] += 1

    def every_group(*accs):
        def pop(block, part, sums):
            both = pltpu.matmul_pop(accs[block * (GROUP // HALF) + part])
            term = both[:, :width] + both[:, width:]
            if block == 0:
                sums[part] = (term, jnp.zeros_like(term))
            else:
                along, across = sums[part]
                along = along + term * waves[cos_at + block : cos_at + block + 1, :]
                across = across + term * waves[sin_at + block : sin_at + block + 1, :]
                sums[part] = (along, across)

        def drain(both, parts, sums):
            for part in range(parts):
                for block in both:
                    pop(block, part, sums)

        for group in range(rows // GROUP):
            tops = [group * GROUP + part * HALF for part in range(GROUP // HALF)]
            sums = [None] * len(tops)
            ready, late = [], []
            pushed = [0, 0]
            pltpu.matmul_push_rhs(edge, 1, 0)
            for unit in range(2):
                push_next(unit, pushed)
            for number, members in enumerate(sets):
                if group == 0:
                    copies[number].wait()
                if number == 0:
                    for part, top in enumerate(tops):
                        lhs = piece(pl.ds(top, HALF), 0)
                        pltpu.matmul_acc_lhs(accs[part], lhs, load_staged_rhs=None if part else 1)
                for step in range(steps_count):
                    fresh = [None, None]
                    for unit in range(2):
                        if used(members, step, unit):
                            fresh[unit] = (pushed[unit] - 1) % 2
                            push_next(unit, pushed)
                    for pair in range(members[0], members[-1] + 1, 2):
                        both = [block for block in (pair, pair + 1) if block in members]
                        for part, top in enumerate(tops):
                            for block in both:
                                start = block * SPAN + step * MXU
                                if start < samples:
                                    acc = accs[block * len(tops) + part]
                                    lhs = piece(pl.ds(top, HALF), start)
                                    pltpu.matmul_acc_lhs(acc, lhs, load_staged_rhs=fresh[block % 2])
                                    fresh[block % 2] = None
                        if ready:
                            drain(ready.pop(0), len(tops), sums)
                        if step == steps_count - 1:
                            late.append(both)
                while ready:
                    drain(ready.pop(0), len(tops), sums)
                ready, late = late, []
            for both in ready:
                drain(both, len(tops), sums)
            for part, top in enumerate(tops):
                finish(top, *sums[part])

    pl.run_scoped(every_group, *accs)
    out[:rows, :] = ordered[...].astype(out.dtype)
    owner = channels[...] // (CH_DEV * ncols)
    local = owner * CH_DEV + channels[...] % CH_DEV
    if counts:
        local = jnp.where(iota((1, slots), 1) < counts[0][0, 0], local, -1)
    local = local.astype(jnp.float32)
    local = jnp.concatenate([local, jnp.zeros((1, LANES - slots), jnp.float32)], axis=1)
    local = jnp.broadcast_to(local, (TILE, LANES))
    labels = jnp.take_along_axis(local, iota((TILE, LANES), 1) % slots, axis=1)
    out[rows:, :] = labels.astype(out.dtype)


def whiten(raw_files, file_channels, reader_counts, fir_taps, band_bins, ncols):
    slots, _, records, samples = raw_files.shape
    rows = slots * records
    bins = band_bins.shape[0]
    taps = fir_taps.shape[0]
    width = 2 * bins
    counts = [] if slots == CH_DEV else [reader_counts]
    anywhere = pl.BlockSpec(memory_space=pl.ANY)
    depth = (LANES // DEC + taps // DEC - 1 + TILE - 1) // TILE * TILE
    table_rows = depth + 2 * (SPAN // LANES) + 2 * TILE
    return pl.pallas_call(
        functools.partial(whiten_kernel, ncols, records),
        out_shape=jax.ShapeDtypeStruct((rows + TILE, width), jnp.bfloat16),
        in_specs=[anywhere] * 4 + [pl.BlockSpec(memory_space=pltpu.SMEM)] * len(counts),
        out_specs=pl.BlockSpec(memory_space=pltpu.VMEM),
        scratch_shapes=[
            pltpu.VMEM((rows, samples), jnp.bfloat16),
            pltpu.VMEM((1, taps), jnp.float32),
            pltpu.VMEM((1, bins), jnp.int32),
            pltpu.VMEM((1, slots), jnp.int32),
            pltpu.VMEM((table_rows, width), jnp.float32),
            pltpu.VMEM((rows, width), jnp.float32),
            pltpu.SemaphoreType.DMA((len(CUTS) + 4,)),
        ],
        compiler_params=pltpu.CompilerParams(vmem_limit_bytes=SMALL),
        cost_estimate=pl.CostEstimate(
            flops=4 * rows * samples * width, bytes_accessed=2 * rows * samples, transcendentals=0
        ),
        name="whiten",
    )(
        *(
            pltpu.with_memory_space_constraint(x, pltpu.HBM)
            for x in (
                raw_files.reshape(rows, samples),
                fir_taps.reshape(1, -1),
                band_bins.reshape(1, -1),
                file_channels.reshape(1, -1),
            )
        ),
        *counts,
    )


def gather_channels(packets, first, count, slots, records):
    held = LANES // slots
    picks = []
    for start in range(0, len(packets), held):
        group = packets[start : start + held]
        lane = iota((1, LANES), 1) // slots
        label = jnp.full((1, LANES), -1.0, jnp.float32)
        for index, packet in enumerate(group):
            row = packet[slots * records : slots * records + TILE, :].astype(jnp.float32)[:1]
            label = jnp.where(lane == index, row, label)
        wanted = (iota((count, 1), 0) + first).astype(jnp.float32)
        pick = (wanted == label).astype(jnp.float32).astype(jnp.bfloat16)
        picks.append(pick[:, : len(group) * slots])
    data = [
        jnp.concatenate([packet[e * slots : (e + 1) * slots, :] for e in range(records)], axis=1)
        for packet in packets
    ]
    return dot(jnp.concatenate(picks, axis=1), jnp.concatenate(data, axis=0))


def own_kernel(records, slots, *refs):
    packets, out = refs[:-1], refs[-1]
    width = out.shape[1]
    placed = gather_channels(packets, lax.axis_index("row") * CH_DEV, CH_DEV, slots, records)
    for e in range(records):
        out[e * CH_DEV : (e + 1) * CH_DEV, :] = placed[:, e * width : (e + 1) * width].astype(out.dtype)


def own_block(packets, records, slots):
    vmem = pl.BlockSpec(memory_space=pltpu.VMEM)
    return pl.pallas_call(
        functools.partial(own_kernel, records, slots),
        out_shape=jax.ShapeDtypeStruct((CH_DEV * records, packets[0].shape[1]), packets[0].dtype),
        in_specs=[vmem] * len(packets),
        out_specs=vmem,
        compiler_params=pltpu.CompilerParams(vmem_limit_bytes=SMALL),
        name="own",
    )(*packets)


def stack_piece(records, left, right_re, right_im, turned, tile):
    width = left.shape[1]
    half = width // 2
    count = right_re.shape[1]
    low = iota((1, width), 1) < half
    piece = left[...].astype(jnp.float32) * (1.0 / records)
    swapped = pltpu.roll(piece, half, 1)
    turned[0] = piece
    turned[1] = jnp.where(low, swapped, -swapped)

    @pl.loop(0, count // BLOCK)
    def _(j):
        rows = pl.ds(pl.multiple_of(j * BLOCK, BLOCK), BLOCK)
        res = [right_re[e, rows, :] for e in range(records)]
        ims = [right_im[e, rows, :] for e in range(records)]
        for k in range(CH_DEV):
            terms = [None] * CHAINS
            for e in range(records):
                at = slice(e * CH_DEV + k, e * CH_DEV + k + 1)
                for side, right in ((0, res[e]), (1, ims[e])):
                    wide = jnp.broadcast_to(turned[side, at, :], (TILE, width)).astype(jnp.bfloat16)
                    term = jnp.concatenate([wide] * (BLOCK // TILE), axis=0) * right
                    chain = (2 * e + side) % CHAINS
                    terms[chain] = term if terms[chain] is None else terms[chain] + term
            while len(terms) > 1:
                terms = [a + b for a, b in zip(terms[::2], terms[1::2])] + terms[len(terms) // 2 * 2 :]
            tile[k, rows, :] = terms[0]


def first_kernel(records, slots, *refs):
    packets = refs[:-5]
    left, tile, right_re, right_im, turned = refs[-5:]
    width = left.shape[1]
    half = width // 2
    count = right_re.shape[1]
    low = iota((1, width), 1) < half
    for start in range(0, count, BLOCK):
        placed = gather_channels(packets, start, BLOCK, slots, records)
        for e in range(records):
            one = placed[:, e * width : (e + 1) * width]
            swapped = pltpu.roll(one, half, 1)
            right_re[e, start : start + BLOCK, :] = jnp.where(low, one, swapped).astype(right_re.dtype)
            right_im[e, start : start + BLOCK, :] = jnp.where(low, swapped, one).astype(right_im.dtype)
    stack_piece(records, left, right_re, right_im, turned, tile)


def next_kernel(records, left, right_re, right_im, tile, turned):
    stack_piece(records, left, right_re, right_im, turned, tile)


def last_kernel(records, shifts, made, *refs):
    done, refs = refs[:made], refs[made:]
    lefts, refs = refs[: len(shifts) - made], refs[len(shifts) - made :]
    right_re, right_im, out, turned, tiles, sems = refs
    mine = lax.axis_index("col")
    copies = []

    def send(tile, index):
        place = partner(mine, shifts[index], len(shifts), True)
        copies.append(pltpu.make_async_copy(tile, out.at[pl.ds(place * CH_DEV, CH_DEV)], sems.at[index]))
        copies[-1].start()

    for index, tile in enumerate(done):
        send(tile, index)
    for index, left in enumerate(lefts):
        stack_piece(records, left, right_re, right_im, turned, tiles.at[index])
        send(tiles.at[index], made + index)
    for copy in copies:
        copy.wait()


def stacked(packets, lefts, records, slots):
    nrows, ncols = len(packets), len(lefts)
    width = packets[0].shape[1]
    count = nrows * CH_DEV
    vmem = pl.BlockSpec(memory_space=pltpu.VMEM)
    right = jax.ShapeDtypeStruct((records, count, width), jnp.bfloat16)
    tile = jax.ShapeDtypeStruct((CH_DEV, count, width), jnp.bfloat16)
    turned = pltpu.VMEM((2, CH_DEV * records, width), jnp.float32)
    params = pltpu.CompilerParams(vmem_limit_bytes=SMALL)

    def cost(pieces):
        work = 4 * CH_DEV * count * width * records * pieces
        return pl.CostEstimate(flops=256 * work, bytes_accessed=tile.size * 2 * pieces, transcendentals=0)

    first, right_re, right_im = pl.pallas_call(
        functools.partial(first_kernel, records, slots),
        out_shape=(tile, right, right),
        in_specs=[vmem] * (nrows + 1),
        out_specs=(vmem,) * 3,
        scratch_shapes=[turned],
        compiler_params=params,
        cost_estimate=cost(1),
        name="first",
    )(*packets, lefts[0][1])
    tiles = [first]
    early = min(EARLY, ncols - 2)
    for _, left in lefts[1 : 1 + early]:
        tiles.append(
            pl.pallas_call(
                functools.partial(next_kernel, records),
                out_shape=tile,
                in_specs=[vmem] * 3,
                out_specs=vmem,
                scratch_shapes=[turned],
                compiler_params=params,
                cost_estimate=cost(1),
                name="next",
            )(left, right_re, right_im)
        )
    others = [left for _, left in lefts[1 + early :]]
    return pl.pallas_call(
        functools.partial(last_kernel, records, [shift for shift, _ in lefts], len(tiles)),
        out_shape=jax.ShapeDtypeStruct((ncols * CH_DEV, count, width), jnp.bfloat16),
        in_specs=[vmem] * (len(tiles) + len(others) + 2),
        out_specs=pl.BlockSpec(memory_space=pl.ANY),
        scratch_shapes=[
            turned,
            pltpu.VMEM((len(others), CH_DEV, count, width), jnp.bfloat16),
            pltpu.SemaphoreType.DMA((ncols,)),
        ],
        compiler_params=params,
        cost_estimate=cost(len(others)),
        name="last",
    )(*tiles, *others, right_re, right_im)


def partner(index, shift, size, back=False):
    if size & (size - 1) == 0:
        return index ^ shift
    return (index + (size - shift if back else shift)) % size


def shifted(block, axis, order):
    size = lax.axis_size(axis)
    shifts = list(order) if len(order) == size - 1 else list(range(1, size))
    return [(0, block)] + [
        (s, lax.ppermute(block, axis, [(i, partner(i, s, size)) for i in range(size)])) for s in shifts
    ]


def on_device(raw_files, file_channels, reader_counts, fir_taps, band_bins):
    ncols = lax.axis_size("col")
    slots, _, records, _ = raw_files.shape
    packet = whiten(raw_files, file_channels, reader_counts, fir_taps, band_bins, ncols)
    packets = [block for _, block in shifted(packet, "row", ROW_ORDER)]
    own = own_block(packets, records, slots)
    lefts = shifted(own, "col", COL_ORDER)
    lefts = [lefts[0]] + sorted(lefts[1:], key=lambda left: USE_ORDER.index(left[0]) if left[0] in USE_ORDER else 9)
    return stacked(packets, lefts, records, slots)[:, None, :, :]


def solution(mesh):
    return jax.shard_map(
        on_device,
        mesh=mesh,
        in_specs=(
            P(("groups", "row"), "col", None, None),
            P(("groups", "row"), "col"),
            P(("groups", "row"), "col"),
            P(),
            P(),
        ),
        out_specs=P(("groups", "row"), "col", None, None),
        check_vma=False,
    )
```

time: 20.2 us -> 18.3 us (0.906)
  Pallas kernels: 7.56 us -> 5.08 us
  waiting for transfers between devices: 4.71 us -> 5.38 us
    pallas_call x3 -> x4, Pallas kernels: 4.66 us -> 2.58 us  [the longest x1 1.45 us: stacked(): pl.pallas_call(functools.partial(last_kernel, records, [shift for shift,...]
    ppermute x6, waiting for transfers between devices: 4.71 us -> 5.38 us  [shifted(): lax.ppermute(block, axis, [(i, partner(i, s, size)) for i in range(size)])]
    pallas_call x1, Pallas kernels: 2.9 us -> 2.49 us  [whiten(): pl.pallas_call(functools.partial(whiten_kernel, ncols, records), out_shap...]
  transfers between devices with their start and end apart: 6 -> 6, of which waited for: 4 -> 5; matrix products, arithmetic and copies ran while one was open for 0% -> 0% of each run, Pallas kernels for 8% -> 6%
where the time goes in v4:
time: 18.3 us; the launch traced here: 18.1 us
  starting transfers between devices  7.65 us (42%)
  waiting for transfers between devices  5.38 us (29%)
  Pallas kernels  5.08 us (28%)
    ppermute x6, starting transfers between devices, shifted(): lax.ppermute(block, axis, [(i, partner(i, s, size)) for i in range(size)])  7.65 us
    ppermute x6, waiting for transfers between devices, shifted(): lax.ppermute(block, axis, [(i, partner(i, s, size)) for i in range(size)])  5.38 us
    pallas_call x1, Pallas kernels, whiten(): pl.pallas_call(functools.partial(whiten_kernel, ncols, records), out_shap...  2.49 us
    pallas_call x1, Pallas kernels, stacked(): pl.pallas_call(functools.partial(last_kernel, records, [shift for shift,...  1.45 us
    pallas_call x1, Pallas kernels, stacked(): pl.pallas_call(functools.partial(first_kernel, records, slots), out_shape...  0.63 us
    pallas_call x1, Pallas kernels, stacked(): pl.pallas_call(functools.partial(next_kernel, records), out_shape=tile, i...  0.38 us
  transfers between devices with their start and end apart: 6, of which 5 were waited for; matrix products, arithmetic and copies ran while one was open for 0% of the time, Pallas kernels for 6%

profile of v4, /device:TPU:0, one launch (start us, length us, event | category | flops | bytes accessed | tf_op | source)
XLA Modules:
  0.0 18.1 jit_solution(6988274691533114770)
XLA Ops:
  0.0 2.5 %whiten.1.refs_0_ = bf16[144,128]{1,0:T(8,128)(2,1)S(1)} custom-call(bf16[128,12000]{1,0:T(8,128)(2,1)} %bitcast.7, f32[1,32]{1,0:T(1,128)} %bitcast.8, s32[1,64]{1,0:T(1,128)} %bitcast.9, s32[1,16]{1,0:T(1,128)} %bitcast.10), custom_call_target="tpu_custom_call" | custom-call | flops 786432000 | bytes 3072000 | tf_op jit(solution)/shard_map/whiten/pallas_call | solution.py:257
  2.5 5.1 %collective-permute-start.2 = (bf16[144,128]{1,0:T(8,128)(2,1)S(1)}, bf16[144,128]{1,0:T(8,128)(2,1)S(1)}, u32[]{:S(2)}, u32[]{:S(2)}) collective-permute-start(bf16[144,128]{1,0:T(8,128)(2,1)S(1)} %whiten.1.refs_0_), channel_id=1, source_target_pairs={{0,12},{4,8},{8,4},{12,0},{1,13},{5,9},{9,5},{13,1},{2,14},{6,10},... | collective-permute-start | bytes 110600 | tf_op jit(solution)/shard_map/ppermute | solution.py:467
  7.6 0.0 collective-permute-start.1
  7.6 0.6 %collective-permute-start = (bf16[144,128]{1,0:T(8,128)(2,1)S(1)}, bf16[144,128]{1,0:T(8,128)(2,1)S(1)}, u32[]{:S(2)}, u32[]{:S(2)}) collective-permute-start(bf16[144,128]{1,0:T(8,128)(2,1)S(1)} %whiten.1.refs_0_), channel_id=1, source_target_pairs={{0,4},{4,0},{8,12},{12,8},{1,5},{5,1},{9,13},{13,9},{2,6},{6,2},{1... | collective-permute-start | bytes 110600 | tf_op jit(solution)/shard_map/ppermute | solution.py:467
  8.3 1.3 %collective-permute-done.2.refs_3_ = bf16[144,128]{1,0:T(8,128)(2,1)S(1)} collective-permute-done((bf16[144,128]{1,0:T(8,128)(2,1)S(1)}, bf16[144,128]{1,0:T(8,128)(2,1)S(1)}, u32[]{:S(2)}, u32[]{:S(2)}) %collective-permute-start.2) | collective-permute-done | bytes 36896 | tf_op jit(solution)/shard_map/ppermute | solution.py:467
  9.6 2.9 %collective-permute-done.1.refs_2_ = bf16[144,128]{1,0:T(8,128)(2,1)S(1)} collective-permute-done((bf16[144,128]{1,0:T(8,128)(2,1)S(1)}, bf16[144,128]{1,0:T(8,128)(2,1)S(1)}, u32[]{:S(2)}, u32[]{:S(2)}) %collective-permute-start.1) | collective-permute-done | bytes 36896 | tf_op jit(solution)/shard_map/ppermute | solution.py:467
  12.5 0.0 collective-permute-done.refs_1_
  12.5 0.1 own.1.refs_4_
  12.6 0.0 collective-permute-start.5
  12.6 1.6 %collective-permute-start.4 = (bf16[128,128]{1,0:T(8,128)(2,1)S(1)}, bf16[128,128]{1,0:T(8,128)(2,1)S(1)}, u32[]{:S(2)}, u32[]{:S(2)}) collective-permute-start(bf16[128,128]{1,0:T(8,128)(2,1)S(1)} %own.1.refs_4_), channel_id=1, source_target_pairs={{0,2},{1,3},{2,0},{3,1},{4,6},{5,7},{6,4},{7,5},{8,10},{9,11},{10,... | collective-permute-start | bytes 98312 | tf_op jit(solution)/shard_map/ppermute | solution.py:467
  14.2 0.3 %collective-permute-start.3 = (bf16[128,128]{1,0:T(8,128)(2,1)S(1)}, bf16[128,128]{1,0:T(8,128)(2,1)S(1)}, u32[]{:S(2)}, u32[]{:S(2)}) collective-permute-start(bf16[128,128]{1,0:T(8,128)(2,1)S(1)} %own.1.refs_4_), channel_id=1, source_target_pairs={{0,1},{1,0},{2,3},{3,2},{4,5},{5,4},{6,7},{7,6},{8,9},{9,8},{10,11... | collective-permute-start | bytes 98312 | tf_op jit(solution)/shard_map/ppermute | solution.py:467
  14.5 0.6 %first.1 = (bf16[16,64,128]{2,1,0:T(8,128)(2,1)S(1)}, bf16[8,64,128]{2,1,0:T(8,128)(2,1)S(1)}, bf16[8,64,128]{2,1,0:T(8,128)(2,1)S(1)}) custom-call(bf16[144,128]{1,0:T(8,128)(2,1)S(1)} %whiten.1.refs_0_, bf16[144,128]{1,0:T(8,128)(2,1)S(1)} %collective-permute-done.refs_1_, bf16[144,128]{1,0:T(8,128)(2,1)S(1)} %collective-permute-done.1.refs_2_, ...), custom_call_target="tpu_custom_call" | custom-call | flops 1073741824 | bytes 262144 | tf_op jit(solution)/shard_map/first/pallas_call | solution.py:415
  15.1 0.3 %collective-permute-done.3.left = bf16[128,128]{1,0:T(8,128)(2,1)S(1)} collective-permute-done((bf16[128,128]{1,0:T(8,128)(2,1)S(1)}, bf16[128,128]{1,0:T(8,128)(2,1)S(1)}, u32[]{:S(2)}, u32[]{:S(2)}) %collective-permute-start.3) | collective-permute-done | bytes 32800 | tf_op jit(solution)/shard_map/ppermute | solution.py:467
  15.4 0.4 %next.1.refs_1_ = bf16[16,64,128]{2,1,0:T(8,128)(2,1)S(1)} custom-call(bf16[128,128]{1,0:T(8,128)(2,1)S(1)} %collective-permute-done.3.left, bf16[8,64,128]{2,1,0:T(8,128)(2,1)S(1)} %get-tuple-element.9.right_re.refs_4_, bf16[8,64,128]{2,1,0:T(8,128)(2,1)S(1)} %get-tuple-element.10.right_im.refs_5_), custom_call_target="tpu_custom_call" | custom-call | flops 1073741824 | bytes 262144 | tf_op jit(solution)/shard_map/next/pallas_call | solution.py:429
  15.8 0.5 %collective-permute-done.5.refs_3_ = bf16[128,128]{1,0:T(8,128)(2,1)S(1)} collective-permute-done((bf16[128,128]{1,0:T(8,128)(2,1)S(1)}, bf16[128,128]{1,0:T(8,128)(2,1)S(1)}, u32[]{:S(2)}, u32[]{:S(2)}) %collective-permute-start.5) | collective-permute-done | bytes 32800 | tf_op jit(solution)/shard_map/ppermute | solution.py:467
  16.3 0.4 %collective-permute-done.4.refs_2_ = bf16[128,128]{1,0:T(8,128)(2,1)S(1)} collective-permute-done((bf16[128,128]{1,0:T(8,128)(2,1)S(1)}, bf16[128,128]{1,0:T(8,128)(2,1)S(1)}, u32[]{:S(2)}, u32[]{:S(2)}) %collective-permute-start.4) | collective-permute-done | bytes 32800 | tf_op jit(solution)/shard_map/ppermute | solution.py:467
  16.7 1.5 %last.1 = bf16[64,64,128]{2,1,0:T(8,128)(2,1)} custom-call(bf16[16,64,128]{2,1,0:T(8,128)(2,1)S(1)} %get-tuple-element.8.refs_0_, bf16[16,64,128]{2,1,0:T(8,128)(2,1)S(1)} %next.1.refs_1_, bf16[128,128]{1,0:T(8,128)(2,1)S(1)} %collective-permute-done.4.refs_2_, bf16[128,128]{1,0:T(8,128)(2,1)S(1)} %collective-permute-done.5.refs_3_, ...), custom_call_target="tpu_custom_call" | custom-call | flops 2147483648 | bytes 524288 | tf_op jit(solution)/shard_map/last/pallas_call | solution.py:441
Async XLA Ops:
  2.5 7.1 %collective-permute-start.2 = (bf16[144,128]{1,0:T(8,128)(2,1)S(1)}, bf16[144,128]{1,0:T(8,128)(2,1)S(1)}, u32[]{:S(2)}, u32[]{:S(2)}) collective-permute-start(bf16[144,128]{1,0:T(8,128)(2,1)S(1)} %whiten.1.refs_0_), channel_id=1, source_target_pairs={{0,12},{4,8},{8,4},{12,0},{1,13},{5,9},{9,5},{13,1},{2,14},{6,10},... | collective-permute-start | bytes 110600 | tf_op jit(solution)/shard_map/ppermute | solution.py:467
  7.6 4.9 %collective-permute-start.1 = (bf16[144,128]{1,0:T(8,128)(2,1)S(1)}, bf16[144,128]{1,0:T(8,128)(2,1)S(1)}, u32[]{:S(2)}, u32[]{:S(2)}) collective-permute-start(bf16[144,128]{1,0:T(8,128)(2,1)S(1)} %whiten.1.refs_0_), channel_id=1, source_target_pairs={{0,8},{4,12},{8,0},{12,4},{1,9},{5,13},{9,1},{13,5},{2,10},{6,14},... | collective-permute-start | bytes 110600 | tf_op jit(solution)/shard_map/ppermute | solution.py:467
  7.6 4.9 %collective-permute-start = (bf16[144,128]{1,0:T(8,128)(2,1)S(1)}, bf16[144,128]{1,0:T(8,128)(2,1)S(1)}, u32[]{:S(2)}, u32[]{:S(2)}) collective-permute-start(bf16[144,128]{1,0:T(8,128)(2,1)S(1)} %whiten.1.refs_0_), channel_id=1, source_target_pairs={{0,4},{4,0},{8,12},{12,8},{1,5},{5,1},{9,13},{13,9},{2,6},{6,2},{1... | collective-permute-start | bytes 110600 | tf_op jit(solution)/shard_map/ppermute | solution.py:467
  12.6 3.7 %collective-permute-start.5 = (bf16[128,128]{1,0:T(8,128)(2,1)S(1)}, bf16[128,128]{1,0:T(8,128)(2,1)S(1)}, u32[]{:S(2)}, u32[]{:S(2)}) collective-permute-start(bf16[128,128]{1,0:T(8,128)(2,1)S(1)} %own.1.refs_4_), channel_id=1, source_target_pairs={{0,3},{1,2},{2,1},{3,0},{4,7},{5,6},{6,5},{7,4},{8,11},{9,10},{10,... | collective-permute-start | bytes 98312 | tf_op jit(solution)/shard_map/ppermute | solution.py:467
  12.6 4.0 %collective-permute-start.4 = (bf16[128,128]{1,0:T(8,128)(2,1)S(1)}, bf16[128,128]{1,0:T(8,128)(2,1)S(1)}, u32[]{:S(2)}, u32[]{:S(2)}) collective-permute-start(bf16[128,128]{1,0:T(8,128)(2,1)S(1)} %own.1.refs_4_), channel_id=1, source_target_pairs={{0,2},{1,3},{2,0},{3,1},{4,6},{5,7},{6,4},{7,5},{8,10},{9,11},{10,... | collective-permute-start | bytes 98312 | tf_op jit(solution)/shard_map/ppermute | solution.py:467
  14.2 1.2 %collective-permute-start.3 = (bf16[128,128]{1,0:T(8,128)(2,1)S(1)}, bf16[128,128]{1,0:T(8,128)(2,1)S(1)}, u32[]{:S(2)}, u32[]{:S(2)}) collective-permute-start(bf16[128,128]{1,0:T(8,128)(2,1)S(1)} %own.1.refs_4_), channel_id=1, source_target_pairs={{0,1},{1,0},{2,3},{3,2},{4,5},{5,4},{6,7},{7,6},{8,9},{9,8},{10,11... | collective-permute-start | bytes 98312 | tf_op jit(solution)/shard_map/ppermute | solution.py:467

commit v5 on v4

--- a/solution.py
+++ b/solution.py
@@ -1,5 +1,4 @@
 import functools
-import math
 
 import jax
 import jax.numpy as jnp
@@ -8,22 +7,24 @@
 from jax.experimental.pallas import tpu as pltpu
 from jax.sharding import PartitionSpec as P
 
+
 CH_DEV = 16
 DEC = 4
 SPAN = 1024
 LANES = 128
 TILE = 16
 BLOCK = 64
-EARLY = 1
-CHAINS = 2
+EARLY = 2
+CHAINS = 4
+PARTS = 1
+USE = (0, 1, 3, 2)
 GROUP = 128
 HALF = 64
 CUTS = (4, 8)
 MXU = 256
 SMALL = 16 << 20
-ROW_ORDER = (1, 2, 3)
-COL_ORDER = (1, 2, 3)
-USE_ORDER = (1, 2, 3)
+ROW_PLANS = {4: ((1, 0, 3, 2), (3, 2, 0, 1), (2, 3, 1, 0))}
+COL_PLANS = {4: ((1, 0, 3, 2), (2, 3, 0, 1), (3, 2, 1, 0))}
 SIN = (6.283185307, -41.341702147, 81.60523051, -76.704495669, 42.014104466, -14.423992009)
 
 
@@ -44,10 +45,6 @@
 
 def dot(a, b):
     return jnp.dot(a, b, preferred_element_type=jnp.float32)
-
-
-def dot_t(a, b):
-    return lax.dot_general(a, b, (((1,), (1,)), ((), ())), preferred_element_type=jnp.float32)
 
 
 def iota(shape, axis):
@@ -327,7 +324,7 @@
     )(*packets)
 
 
-def stack_piece(records, left, right_re, right_im, turned, tile):
+def stack_piece(records, left, right_re, right_im, turned, tile, send=None):
     width = left.shape[1]
     half = width // 2
     count = right_re.shape[1]
@@ -337,23 +334,31 @@
     turned[0] = piece
     turned[1] = jnp.where(low, swapped, -swapped)
 
-    @pl.loop(0, count // BLOCK)
-    def _(j):
-        rows = pl.ds(pl.multiple_of(j * BLOCK, BLOCK), BLOCK)
-        res = [right_re[e, rows, :] for e in range(records)]
-        ims = [right_im[e, rows, :] for e in range(records)]
-        for k in range(CH_DEV):
-            terms = [None] * CHAINS
-            for e in range(records):
-                at = slice(e * CH_DEV + k, e * CH_DEV + k + 1)
-                for side, right in ((0, res[e]), (1, ims[e])):
-                    wide = jnp.broadcast_to(turned[side, at, :], (TILE, width)).astype(jnp.bfloat16)
-                    term = jnp.concatenate([wide] * (BLOCK // TILE), axis=0) * right
-                    chain = (2 * e + side) % CHAINS
-                    terms[chain] = term if terms[chain] is None else terms[chain] + term
-            while len(terms) > 1:
-                terms = [a + b for a, b in zip(terms[::2], terms[1::2])] + terms[len(terms) // 2 * 2 :]
-            tile[k, rows, :] = terms[0]
+    def some(first, number):
+        @pl.loop(0, count // BLOCK)
+        def _(j):
+            rows = pl.ds(pl.multiple_of(j * BLOCK, BLOCK), BLOCK)
+            res = [right_re[e, rows, :] for e in range(records)]
+            ims = [right_im[e, rows, :] for e in range(records)]
+            for k in range(first, first + number):
+                terms = [None] * CHAINS
+                for e in range(records):
+                    at = slice(e * CH_DEV + k, e * CH_DEV + k + 1)
+                    for side, right in ((0, res[e]), (1, ims[e])):
+                        wide = jnp.broadcast_to(turned[side, at, :], (TILE, width)).astype(jnp.bfloat16)
+                        term = jnp.concatenate([wide] * (BLOCK // TILE), axis=0) * right
+                        chain = (2 * e + side) % CHAINS
+                        terms[chain] = term if terms[chain] is None else terms[chain] + term
+                while len(terms) > 1:
+                    terms = [a + b for a, b in zip(terms[::2], terms[1::2])] + terms[len(terms) // 2 * 2 :]
+                tile[k, rows, :] = terms[0]
+
+    if send is None:
+        some(0, CH_DEV)
+    else:
+        for first in range(0, CH_DEV, CH_DEV // PARTS):
+            some(first, CH_DEV // PARTS)
+            send(first, CH_DEV // PARTS)
 
 
 def first_kernel(records, slots, *refs):
@@ -373,27 +378,31 @@
     stack_piece(records, left, right_re, right_im, turned, tile)
 
 
-def next_kernel(records, left, right_re, right_im, tile, turned):
+def next_kernel(records, left, right_re, right_im, after, tile, turned):
+    del after
     stack_piece(records, left, right_re, right_im, turned, tile)
 
 
-def last_kernel(records, shifts, made, *refs):
+def last_kernel(records, plans, made, *refs):
     done, refs = refs[:made], refs[made:]
-    lefts, refs = refs[: len(shifts) - made], refs[len(shifts) - made :]
+    lefts, refs = refs[: len(plans) - made], refs[len(plans) - made :]
     right_re, right_im, out, turned, tiles, sems = refs
     mine = lax.axis_index("col")
     copies = []
 
-    def send(tile, index):
-        place = partner(mine, shifts[index], len(shifts), True)
-        copies.append(pltpu.make_async_copy(tile, out.at[pl.ds(place * CH_DEV, CH_DEV)], sems.at[index]))
+    def send(tile, index, first, number):
+        start = source_of(mine, plans[index]) * CH_DEV + first
+        sem = sems.at[index, first * PARTS // CH_DEV]
+        copies.append(pltpu.make_async_copy(tile.at[pl.ds(first, number)], out.at[pl.ds(start, number)], sem))
         copies[-1].start()
 
     for index, tile in enumerate(done):
-        send(tile, index)
+        send(tile, index, 0, CH_DEV)
     for index, left in enumerate(lefts):
-        stack_piece(records, left, right_re, right_im, turned, tiles.at[index])
-        send(tiles.at[index], made + index)
+        tile = tiles.at[index]
+        stack_piece(
+            records, left, right_re, right_im, turned, tile, functools.partial(send, tile, made + index)
+        )
     for copy in copies:
         copy.wait()
 
@@ -429,24 +438,24 @@
             pl.pallas_call(
                 functools.partial(next_kernel, records),
                 out_shape=tile,
-                in_specs=[vmem] * 3,
+                in_specs=[vmem] * 3 + [pl.BlockSpec(memory_space=pl.ANY)],
                 out_specs=vmem,
                 scratch_shapes=[turned],
                 compiler_params=params,
                 cost_estimate=cost(1),
                 name="next",
-            )(left, right_re, right_im)
+            )(left, right_re, right_im, tiles[-1])
         )
     others = [left for _, left in lefts[1 + early :]]
     return pl.pallas_call(
-        functools.partial(last_kernel, records, [shift for shift, _ in lefts], len(tiles)),
+        functools.partial(last_kernel, records, [targets for targets, _ in lefts], len(tiles)),
         out_shape=jax.ShapeDtypeStruct((ncols * CH_DEV, count, width), jnp.bfloat16),
         in_specs=[vmem] * (len(tiles) + len(others) + 2),
         out_specs=pl.BlockSpec(memory_space=pl.ANY),
         scratch_shapes=[
             turned,
             pltpu.VMEM((len(others), CH_DEV, count, width), jnp.bfloat16),
-            pltpu.SemaphoreType.DMA((ncols,)),
+            pltpu.SemaphoreType.DMA((ncols, PARTS)),
         ],
         compiler_params=params,
         cost_estimate=cost(len(others)),
@@ -454,28 +463,39 @@
     )(*tiles, *others, right_re, right_im)
 
 
-def partner(index, shift, size, back=False):
+def plan_of(size, plans):
+    if size in plans:
+        return plans[size]
     if size & (size - 1) == 0:
-        return index ^ shift
-    return (index + (size - shift if back else shift)) % size
-
-
-def shifted(block, axis, order):
+        return [[i ^ shift for i in range(size)] for shift in range(1, size)]
+    return [[(i + shift) % size for i in range(size)] for shift in range(1, size)]
+
+
+def source_of(index, targets):
+    source = jnp.int32(0)
+    for i, target in enumerate(targets):
+        source = jnp.where(index == target, jnp.int32(i), source)
+    return source
+
+
+def exchanged(block, axis, plans):
     size = lax.axis_size(axis)
-    shifts = list(order) if len(order) == size - 1 else list(range(1, size))
-    return [(0, block)] + [
-        (s, lax.ppermute(block, axis, [(i, partner(i, s, size)) for i in range(size)])) for s in shifts
-    ]
+    return [(list(range(size)), block)] + [(targets, moved(block, axis, targets)) for targets in plan_of(size, plans)]
+
+
+def moved(block, axis, targets):
+    return lax.ppermute(block, axis, list(enumerate(targets)))
 
 
 def on_device(raw_files, file_channels, reader_counts, fir_taps, band_bins):
     ncols = lax.axis_size("col")
     slots, _, records, _ = raw_files.shape
     packet = whiten(raw_files, file_channels, reader_counts, fir_taps, band_bins, ncols)
-    packets = [block for _, block in shifted(packet, "row", ROW_ORDER)]
+    packets = [block for _, block in exchanged(packet, "row", ROW_PLANS)]
     own = own_block(packets, records, slots)
-    lefts = shifted(own, "col", COL_ORDER)
-    lefts = [lefts[0]] + sorted(lefts[1:], key=lambda left: USE_ORDER.index(left[0]) if left[0] in USE_ORDER else 9)
+    lefts = exchanged(own, "col", COL_PLANS)
+    if ncols in COL_PLANS:
+        lefts = [lefts[n] for n in USE]
     return stacked(packets, lefts, records, slots)[:, None, :, :]
 
 

time: 18.3 us -> 18.5 us (1.011)
  starting transfers between devices: 7.65 us -> 7.84 us
    pallas_call x1 -> x2, Pallas kernels: 0.38 us -> 0.76 us  [stacked(): pl.pallas_call(functools.partial(next_kernel, records), out_shape=tile, i...]
    pallas_call x1, Pallas kernels: 1.45 us -> 1.12 us  [stacked(): pl.pallas_call(functools.partial(last_kernel, records, [targets for targe...]
    ppermute x6, starting transfers between devices: 7.65 us -> 7.84 us  [moved(): return lax.ppermute(block, axis, list(enumerate(targets)))]
  transfers between devices with their start and end apart: 6 -> 6, of which waited for: 5 -> 5; matrix products, arithmetic and copies ran while one was open for 0% -> 0% of each run, Pallas kernels for 6% -> 8%
where the time goes in v5:
time: 18.5 us; the launch traced here: 18.4 us
  starting transfers between devices  7.84 us (42%)
  waiting for transfers between devices  5.35 us (29%)
  Pallas kernels  5.13 us (28%)
    ppermute x6, starting transfers between devices, moved(): return lax.ppermute(block, axis, list(enumerate(targets)))  7.84 us
    ppermute x6, waiting for transfers between devices, moved(): return lax.ppermute(block, axis, list(enumerate(targets)))  5.35 us
    pallas_call x1, Pallas kernels, whiten(): pl.pallas_call(functools.partial(whiten_kernel, ncols, records), out_shap...  2.49 us
    pallas_call x1, Pallas kernels, stacked(): pl.pallas_call(functools.partial(last_kernel, records, [targets for targe...  1.12 us
    pallas_call x2, Pallas kernels, stacked(): pl.pallas_call(functools.partial(next_kernel, records), out_shape=tile, i...  0.76 us
    pallas_call x1, Pallas kernels, stacked(): pl.pallas_call(functools.partial(first_kernel, records, slots), out_shape...  0.62 us
  transfers between devices with their start and end apart: 6, of which 5 were waited for; matrix products, arithmetic and copies ran while one was open for 0% of the time, Pallas kernels for 8%

profile of v5, /device:TPU:0, one launch (start us, length us, event | category | flops | bytes accessed | tf_op | source)
XLA Modules:
  0.0 18.4 jit_solution(7896869438209111471)
XLA Ops:
  0.0 2.5 %whiten.1.refs_0_ = bf16[144,128]{1,0:T(8,128)(2,1)S(1)} custom-call(bf16[128,12000]{1,0:T(8,128)(2,1)} %bitcast.7, f32[1,32]{1,0:T(1,128)} %bitcast.8, s32[1,64]{1,0:T(1,128)} %bitcast.9, s32[1,16]{1,0:T(1,128)} %bitcast.10), custom_call_target="tpu_custom_call" | custom-call | flops 786432000 | bytes 3072000 | tf_op jit(solution)/shard_map/whiten/pallas_call | solution.py:254
  2.5 4.1 %collective-permute-start.2 = (bf16[144,128]{1,0:T(8,128)(2,1)S(1)}, bf16[144,128]{1,0:T(8,128)(2,1)S(1)}, u32[]{:S(2)}, u32[]{:S(2)}) collective-permute-start(bf16[144,128]{1,0:T(8,128)(2,1)S(1)} %whiten.1.refs_0_), channel_id=1, source_target_pairs={{0,8},{4,12},{8,4},{12,0},{1,9},{5,13},{9,5},{13,1},{2,10},{6,14},... | collective-permute-start | bytes 110600 | tf_op jit(solution)/shard_map/ppermute | solution.py:487
  6.6 1.1 %collective-permute-start.1 = (bf16[144,128]{1,0:T(8,128)(2,1)S(1)}, bf16[144,128]{1,0:T(8,128)(2,1)S(1)}, u32[]{:S(2)}, u32[]{:S(2)}) collective-permute-start(bf16[144,128]{1,0:T(8,128)(2,1)S(1)} %whiten.1.refs_0_), channel_id=1, source_target_pairs={{0,12},{4,8},{8,0},{12,4},{1,13},{5,9},{9,1},{13,5},{2,14},{6,10},... | collective-permute-start | bytes 110600 | tf_op jit(solution)/shard_map/ppermute | solution.py:487
  7.7 0.5 %collective-permute-start = (bf16[144,128]{1,0:T(8,128)(2,1)S(1)}, bf16[144,128]{1,0:T(8,128)(2,1)S(1)}, u32[]{:S(2)}, u32[]{:S(2)}) collective-permute-start(bf16[144,128]{1,0:T(8,128)(2,1)S(1)} %whiten.1.refs_0_), channel_id=1, source_target_pairs={{0,4},{4,0},{8,12},{12,8},{1,5},{5,1},{9,13},{13,9},{2,6},{6,2},{1... | collective-permute-start | bytes 110600 | tf_op jit(solution)/shard_map/ppermute | solution.py:487
  8.2 1.4 %collective-permute-done.2.refs_3_ = bf16[144,128]{1,0:T(8,128)(2,1)S(1)} collective-permute-done((bf16[144,128]{1,0:T(8,128)(2,1)S(1)}, bf16[144,128]{1,0:T(8,128)(2,1)S(1)}, u32[]{:S(2)}, u32[]{:S(2)}) %collective-permute-start.2) | collective-permute-done | bytes 36896 | tf_op jit(solution)/shard_map/ppermute | solution.py:487
  9.6 1.9 %collective-permute-done.1.refs_2_ = bf16[144,128]{1,0:T(8,128)(2,1)S(1)} collective-permute-done((bf16[144,128]{1,0:T(8,128)(2,1)S(1)}, bf16[144,128]{1,0:T(8,128)(2,1)S(1)}, u32[]{:S(2)}, u32[]{:S(2)}) %collective-permute-start.1) | collective-permute-done | bytes 36896 | tf_op jit(solution)/shard_map/ppermute | solution.py:487
  11.5 0.4 %collective-permute-done.refs_1_ = bf16[144,128]{1,0:T(8,128)(2,1)S(1)} collective-permute-done((bf16[144,128]{1,0:T(8,128)(2,1)S(1)}, bf16[144,128]{1,0:T(8,128)(2,1)S(1)}, u32[]{:S(2)}, u32[]{:S(2)}) %collective-permute-start) | collective-permute-done | bytes 36896 | tf_op jit(solution)/shard_map/ppermute | solution.py:487
  11.9 0.1 own.1.refs_4_
  12.0 1.5 %collective-permute-start.5 = (bf16[128,128]{1,0:T(8,128)(2,1)S(1)}, bf16[128,128]{1,0:T(8,128)(2,1)S(1)}, u32[]{:S(2)}, u32[]{:S(2)}) collective-permute-start(bf16[128,128]{1,0:T(8,128)(2,1)S(1)} %own.1.refs_4_), channel_id=1, source_target_pairs={{0,2},{1,3},{2,0},{3,1},{4,6},{5,7},{6,4},{7,5},{8,10},{9,11},{10,... | collective-permute-start | bytes 98312 | tf_op jit(solution)/shard_map/ppermute | solution.py:487
  13.5 0.0 collective-permute-start.4
  13.5 0.6 %collective-permute-start.3 = (bf16[128,128]{1,0:T(8,128)(2,1)S(1)}, bf16[128,128]{1,0:T(8,128)(2,1)S(1)}, u32[]{:S(2)}, u32[]{:S(2)}) collective-permute-start(bf16[128,128]{1,0:T(8,128)(2,1)S(1)} %own.1.refs_4_), channel_id=1, source_target_pairs={{0,1},{1,0},{2,3},{3,2},{4,5},{5,4},{6,7},{7,6},{8,9},{9,8},{10,11... | collective-permute-start | bytes 98312 | tf_op jit(solution)/shard_map/ppermute | solution.py:487
  14.2 0.6 %first.1 = (bf16[16,64,128]{2,1,0:T(8,128)(2,1)S(1)}, bf16[8,64,128]{2,1,0:T(8,128)(2,1)S(1)}, bf16[8,64,128]{2,1,0:T(8,128)(2,1)S(1)}) custom-call(bf16[144,128]{1,0:T(8,128)(2,1)S(1)} %whiten.1.refs_0_, bf16[144,128]{1,0:T(8,128)(2,1)S(1)} %collective-permute-done.refs_1_, bf16[144,128]{1,0:T(8,128)(2,1)S(1)} %collective-permute-done.1.refs_2_, ...), custom_call_target="tpu_custom_call" | custom-call | flops 1073741824 | bytes 262144 | tf_op jit(solution)/shard_map/first/pallas_call | solution.py:424
  14.8 0.2 %collective-permute-done.3.left = bf16[128,128]{1,0:T(8,128)(2,1)S(1)} collective-permute-done((bf16[128,128]{1,0:T(8,128)(2,1)S(1)}, bf16[128,128]{1,0:T(8,128)(2,1)S(1)}, u32[]{:S(2)}, u32[]{:S(2)}) %collective-permute-start.3) | collective-permute-done | bytes 32800 | tf_op jit(solution)/shard_map/ppermute | solution.py:487
  15.0 0.4 %next.2.after.refs_1_ = bf16[16,64,128]{2,1,0:T(8,128)(2,1)S(1)} custom-call(bf16[128,128]{1,0:T(8,128)(2,1)S(1)} %collective-permute-done.3.left, bf16[8,64,128]{2,1,0:T(8,128)(2,1)S(1)} %get-tuple-element.9.right_re.refs_4_, bf16[8,64,128]{2,1,0:T(8,128)(2,1)S(1)} %get-tuple-element.10.right_im.refs_5_, bf16[16,64,128]{2,1,0:T(8,128)(2,1)S(1)} %get-tuple-element.8.after.refs_0_), custom_call_target="tpu_custom_call" | custom-call | flops 1073741824 | bytes 262144 | tf_op jit(solution)/shard_map/next/pallas_call | solution.py:438
  15.4 1.4 %collective-permute-done.4.left = bf16[128,128]{1,0:T(8,128)(2,1)S(1)} collective-permute-done((bf16[128,128]{1,0:T(8,128)(2,1)S(1)}, bf16[128,128]{1,0:T(8,128)(2,1)S(1)}, u32[]{:S(2)}, u32[]{:S(2)}) %collective-permute-start.4) | collective-permute-done | bytes 32800 | tf_op jit(solution)/shard_map/ppermute | solution.py:487
  16.8 0.4 %next.3.refs_2_ = bf16[16,64,128]{2,1,0:T(8,128)(2,1)S(1)} custom-call(bf16[128,128]{1,0:T(8,128)(2,1)S(1)} %collective-permute-done.4.left, bf16[8,64,128]{2,1,0:T(8,128)(2,1)S(1)} %get-tuple-element.9.right_re.refs_4_, bf16[8,64,128]{2,1,0:T(8,128)(2,1)S(1)} %get-tuple-element.10.right_im.refs_5_, bf16[16,64,128]{2,1,0:T(8,128)(2,1)S(1)} %next.2.after.refs_1_), custom_call_target="tpu_custom_call" | custom-call | flops 1073741824 | bytes 262144 | tf_op jit(solution)/shard_map/next/pallas_call | solution.py:438
  17.2 0.0 collective-permute-done.5.refs_3_
  17.2 1.1 %last.1 = bf16[64,64,128]{2,1,0:T(8,128)(2,1)} custom-call(bf16[16,64,128]{2,1,0:T(8,128)(2,1)S(1)} %get-tuple-element.8.after.refs_0_, bf16[16,64,128]{2,1,0:T(8,128)(2,1)S(1)} %next.2.after.refs_1_, bf16[16,64,128]{2,1,0:T(8,128)(2,1)S(1)} %next.3.refs_2_, bf16[128,128]{1,0:T(8,128)(2,1)S(1)} %collective-permute-done.5.refs_3_, ...), custom_call_target="tpu_custom_call" | custom-call | flops 1073741824 | bytes 262144 | tf_op jit(solution)/shard_map/last/pallas_call | solution.py:450
Async XLA Ops:
  2.5 7.1 %collective-permute-start.2 = (bf16[144,128]{1,0:T(8,128)(2,1)S(1)}, bf16[144,128]{1,0:T(8,128)(2,1)S(1)}, u32[]{:S(2)}, u32[]{:S(2)}) collective-permute-start(bf16[144,128]{1,0:T(8,128)(2,1)S(1)} %whiten.1.refs_0_), channel_id=1, source_target_pairs={{0,8},{4,12},{8,4},{12,0},{1,9},{5,13},{9,5},{13,1},{2,10},{6,14},... | collective-permute-start | bytes 110600 | tf_op jit(solution)/shard_map/ppermute | solution.py:487
  6.6 4.9 %collective-permute-start.1 = (bf16[144,128]{1,0:T(8,128)(2,1)S(1)}, bf16[144,128]{1,0:T(8,128)(2,1)S(1)}, u32[]{:S(2)}, u32[]{:S(2)}) collective-permute-start(bf16[144,128]{1,0:T(8,128)(2,1)S(1)} %whiten.1.refs_0_), channel_id=1, source_target_pairs={{0,12},{4,8},{8,0},{12,4},{1,13},{5,9},{9,1},{13,5},{2,14},{6,10},... | collective-permute-start | bytes 110600 | tf_op jit(solution)/shard_map/ppermute | solution.py:487
  7.7 4.2 %collective-permute-start = (bf16[144,128]{1,0:T(8,128)(2,1)S(1)}, bf16[144,128]{1,0:T(8,128)(2,1)S(1)}, u32[]{:S(2)}, u32[]{:S(2)}) collective-permute-start(bf16[144,128]{1,0:T(8,128)(2,1)S(1)} %whiten.1.refs_0_), channel_id=1, source_target_pairs={{0,4},{4,0},{8,12},{12,8},{1,5},{5,1},{9,13},{13,9},{2,6},{6,2},{1... | collective-permute-start | bytes 110600 | tf_op jit(solution)/shard_map/ppermute | solution.py:487
  12.0 5.2 %collective-permute-start.5 = (bf16[128,128]{1,0:T(8,128)(2,1)S(1)}, bf16[128,128]{1,0:T(8,128)(2,1)S(1)}, u32[]{:S(2)}, u32[]{:S(2)}) collective-permute-start(bf16[128,128]{1,0:T(8,128)(2,1)S(1)} %own.1.refs_4_), channel_id=1, source_target_pairs={{0,2},{1,3},{2,0},{3,1},{4,6},{5,7},{6,4},{7,5},{8,10},{9,11},{10,... | collective-permute-start | bytes 98312 | tf_op jit(solution)/shard_map/ppermute | solution.py:487
  13.5 3.3 %collective-permute-start.4 = (bf16[128,128]{1,0:T(8,128)(2,1)S(1)}, bf16[128,128]{1,0:T(8,128)(2,1)S(1)}, u32[]{:S(2)}, u32[]{:S(2)}) collective-permute-start(bf16[128,128]{1,0:T(8,128)(2,1)S(1)} %own.1.refs_4_), channel_id=1, source_target_pairs={{0,3},{1,2},{2,1},{3,0},{4,7},{5,6},{6,5},{7,4},{8,11},{9,10},{10,... | collective-permute-start | bytes 98312 | tf_op jit(solution)/shard_map/ppermute | solution.py:487
  13.5 1.5 %collective-permute-start.3 = (bf16[128,128]{1,0:T(8,128)(2,1)S(1)}, bf16[128,128]{1,0:T(8,128)(2,1)S(1)}, u32[]{:S(2)}, u32[]{:S(2)}) collective-permute-start(bf16[128,128]{1,0:T(8,128)(2,1)S(1)} %own.1.refs_4_), channel_id=1, source_target_pairs={{0,1},{1,0},{2,3},{3,2},{4,5},{5,4},{6,7},{7,6},{8,9},{9,8},{10,11... | collective-permute-start | bytes 98312 | tf_op jit(solution)/shard_map/ppermute | solution.py:487
